TPU v7x, 32 devices: a whole 2x2x4 slice. The times are simulated.
32 devices in a mesh: grp: 2 (over x), seq: 16 (over z, y, core).
Axes of the slice: x: 2, y: 2, z: 4, core: 2. Of those that a mesh axis runs over, the one named last changes fastest.
Arguments:
- queries: bfloat16 [16384, 1536], P(('grp', 'seq')), parts along dimension 0, may hold values from -26 to 26
- keys_values: bfloat16 [2, 16384, 1536], P(None, ('grp', 'seq')), parts along dimension 1, may hold values from -26 to 26
- segment_ids: int32 [16384], P('grp'), parts along dimension 0, may hold values from 0 to 31, never falling along the last dimension, each value on 1 to 512 neighbouring positions
- route_shard: int32 [16384, 1], P(('grp', 'seq')), parts along dimension 0, may hold values from 0 to 15; in each aligned block of 512 rows (0 to 511, 512 to 1023, ...) at most 64 rows name the same one
- route_slot: int32 [16384], P(('grp', 'seq')), parts along dimension 0, may hold values from 0 to 511
- control_proj: bfloat16 [1536, 3072], replicated, may hold values from -0.15625 to 0.15625
- base_hidden: bfloat16 [16384, 3072], P(('grp', 'seq')), parts along dimension 0, may hold values from -6 to 6
- cotangent: bfloat16 [16384, 3072], P(('grp', 'seq')), parts along dimension 0, may hold values from -1.25 to 1.25
Outputs:
- mixed_hidden: bfloat16 [16384, 3072], P(('grp', 'seq')), parts along dimension 0
- proj_grad: float32 [3072, 3072], P(('grp', 'seq')), parts along dimension 0
There are 2 independent parts, one for each index of `grp`. A program takes and returns all parts, laid end to end along the dimension named above; an argument that names none is the same for every part. Nothing has to cross between parts.
Inputs may be any that keep to these rules, and one draw needn't show every extreme that they name: `segment_ids`: segment numbers never fall along the sequence; each image spans 1 to 512 tokens, one exactly 512. `route_shard`: of the 512 rows of one device, at most 64 name the same base shard; in every draw some device sends exactly 64 rows to one shard.
All inputs are finite; a program needn't handle non-finite values.
Results may differ from a plain program's by a relative error of at most 0.008.
Values may be sent and summed in bfloat16 or wider, within the bound.
No kernel may reach another device: no remote copies, remote signals or barrier semaphores. Data moves between devices by JAX's collectives and lax.ppermute only.
A program may use at most 192 MiB of HBM per device.

v0:
```python
import math

import jax
import jax.numpy as jnp
from jax import lax
from jax.sharding import PartitionSpec as P

HEAD = 128
SEG_MAX = 512


def with_halo(value, sides, width):
    for axis, dim in sides:
        size, length = (lax.axis_size(axis), value.shape[dim])
        up = [(i, (i + 1) % size) for i in range(size - 1)]
        down = [(j, i) for i, j in up]
        last = lax.slice_in_dim(value, length - width, length, axis=dim)
        first = lax.slice_in_dim(value, 0, width, axis=dim)
        before = lax.ppermute(last, axis, up)
        after = lax.ppermute(first, axis, down)
        value = jnp.concatenate([before, value, after], axis=dim)
    return value


def attend_group(query_heads, key_heads, value_heads, keep_mask):
    scores = jnp.einsum(
        "qhd,khd->hqk", query_heads, key_heads, preferred_element_type=jnp.float32
    ) * HEAD ** (-0.5)
    scores = jnp.where(keep_mask, scores, -1e30)
    row_peak = jnp.max(scores, axis=2, keepdims=True)
    exp_scores = jnp.where(keep_mask, jnp.exp(scores - row_peak), 0.0)
    attn_weights = (exp_scores / jnp.sum(exp_scores, axis=2, keepdims=True)).astype(jnp.bfloat16)
    return jnp.einsum("hqk,khd->qhd", attn_weights, value_heads, preferred_element_type=jnp.float32)


def attend_block(query_rows, near_pairs, query_seg, key_seg):
    row_count = query_rows.shape[0]
    head_count = query_rows.shape[1] // HEAD
    group_size = math.gcd(head_count, 4)
    query_heads = query_rows.reshape(row_count, head_count, HEAD)
    key_heads = near_pairs[0].reshape(-1, head_count, HEAD)
    value_heads = near_pairs[1].reshape(-1, head_count, HEAD)
    keep_mask = (query_seg[:, None] == key_seg[None, :])[None]
    pieces = []
    for first_head in range(0, head_count, group_size):
        last_head = first_head + group_size
        pieces.append(
            attend_group(
                query_heads[:, first_head:last_head],
                key_heads[:, first_head:last_head],
                value_heads[:, first_head:last_head],
                keep_mask,
            )
        )
    result = jnp.concatenate(pieces, axis=1)
    return result.reshape(row_count, head_count * HEAD).astype(jnp.bfloat16)


def body(
    queries, keys_values, segment_ids, route_shard, route_slot, control_proj, base_hidden, cotangent
):
    row_count = queries.shape[0]
    model_width = control_proj.shape[1]
    shard_count = lax.axis_size("seq")
    shard_index = lax.axis_index("seq")
    capacity = 2 * row_count // shard_count
    margined = with_halo(keys_values, (("seq", 1),), SEG_MAX)
    padded_seg = jnp.pad(segment_ids, (SEG_MAX, SEG_MAX), constant_values=-1)
    first_row = shard_index * row_count
    query_seg = lax.dynamic_slice_in_dim(segment_ids, first_row, row_count)
    key_seg = lax.dynamic_slice_in_dim(padded_seg, first_row, row_count + 2 * SEG_MAX)
    attended = attend_block(queries, margined, query_seg, key_seg)
    target_shard = route_shard[:, 0]
    one_hot = (target_shard[:, None] == jnp.arange(shard_count, dtype=jnp.int32)[None, :]).astype(
        jnp.int32
    )
    slot_rank = jnp.sum((jnp.cumsum(one_hot, axis=0) - 1) * one_hot, axis=1)
    flat_place = target_shard * capacity + slot_rank
    slot_count = shard_count * capacity
    place_mask = flat_place[None, :] == jnp.arange(slot_count, dtype=jnp.int32)[:, None]
    placement = place_mask.astype(jnp.bfloat16)
    occupied = jnp.sum(place_mask.astype(jnp.int32), axis=1)
    slot_values = jnp.sum(jnp.where(place_mask, route_slot[None, :], 0), axis=1)
    slot_table = jnp.where(occupied > 0, slot_values, -1).reshape(shard_count, capacity)
    residual = jnp.dot(attended, control_proj, preferred_element_type=jnp.float32).astype(
        jnp.bfloat16
    )
    outgoing = (
        jnp.dot(placement, residual, preferred_element_type=jnp.float32)
        .astype(jnp.bfloat16)
        .reshape(shard_count, capacity, model_width)
    )
    incoming, incoming_slots = (
        lax.all_to_all(outgoing, "seq", split_axis=0, concat_axis=0, tiled=True),
        lax.all_to_all(slot_table, "seq", split_axis=0, concat_axis=0, tiled=True),
    )
    flat_slots = incoming_slots.reshape(-1)
    landing_hot = (flat_slots[None, :] == jnp.arange(row_count, dtype=jnp.int32)[:, None]).astype(
        jnp.bfloat16
    )
    added = jnp.dot(
        landing_hot, incoming.reshape(-1, model_width), preferred_element_type=jnp.float32
    )
    mixed_hidden = (base_hidden.astype(jnp.float32) + added).astype(jnp.bfloat16)
    picked = jnp.where(
        (flat_slots >= 0)[:, None],
        cotangent[jnp.maximum(flat_slots, 0)],
        jnp.zeros((), jnp.bfloat16),
    )
    returned = lax.all_to_all(
        picked.reshape(shard_count, capacity, model_width),
        "seq",
        split_axis=0,
        concat_axis=0,
        tiled=True,
    )
    right_rows = returned.reshape(-1, model_width)[flat_place]
    proj_grad = lax.psum_scatter(
        jnp.einsum("th,td->hd", attended, right_rows, preferred_element_type=jnp.float32),
        "seq",
        scatter_dimension=0,
        tiled=True,
    )
    return (mixed_hidden, proj_grad)


def solution(mesh):
    placed = (
        P(("grp", "seq"), None),
        P(None, ("grp", "seq"), None),
        P("grp"),
        P(("grp", "seq"), None),
        P(("grp", "seq")),
        P(),
        P(("grp", "seq"), None),
        P(("grp", "seq"), None),
    )
    return jax.shard_map(
        body,
        mesh=mesh,
        in_specs=placed,
        out_specs=(P(("grp", "seq"), None), P(("grp", "seq"), None)),
        check_vma=False,
    )
```

profile of v0, /device:TPU:10, one launch (start us, length us, event | category | flops | bytes accessed | tf_op | source)
XLA Modules:
  0.0 574.1 jit_solution(8414794333630290842)
XLA Ops:
  21.4 5.4 all-to-all-start
  31.0 54.5 %all-to-all-done = s32[16,1,64]{2,1,0:T(1,128)S(1)} async-done(((s32[16,1,64]{2,1,0:T(1,128)}), s32[16,1,64]{2,1,0:T(1,128)S(1)}, u32[]{:S(2)}, u32[]{:S(2)}) %all-to-all-start) | async-done | bytes 4128 | tf_op jit(solution)/shard_map/all_to_all | solution.py:95
  85.5 6.8 %gather_fusion = bf16[1024,3072]{1,0:T(8,128)(2,1)} fusion(bf16[512,3072]{1,0:T(8,128)(2,1)S(1)} %copy-done, s32[1024]{0:T(1024)S(1)} %broadcast_clamp_fusion), kind=kCustom, calls=%fused_computation | custom fusion | bytes 12587008 | tf_op jit(solution)/shard_map/gather | solution.py:107
  92.3 5.9 %broadcast_select_fusion = bf16[16,64,3072]{2,1,0:T(8,128)(2,1)} fusion(bf16[16,64,3072]{2,1,0:T(8,128)(2,1)} %bitcast.87, pred[16,64]{1,0:T(8,128)(4,1)S(1)} %compare_bitcast_fusion), kind=kLoop, calls=%fused_computation.28 | loop fusion | flops 3145728 | bytes 12583936 | tf_op jit(solution)/shard_map/jit(_where)/select_n | solution.py:105
  98.2 5.6 all-to-all-start.2
  104.0 7.6 %pad_maximum_fusion = bf16[2,1536,1536]{1,2,0:T(8,128)(2,1)} fusion(bf16[2,512,1536]{1,2,0:T(8,128)(2,1)} %collective-permute-done.1, bf16[2,512,1536]{1,2,0:T(8,128)(2,1)S(1)} %copy-done.2, bf16[2,512,1536]{1,2,0:T(8,128)(2,1)} %collective-permute-done), kind=kLoop, calls=%fused_computation.17 | loop fusion | flops 28311552 | bytes 18874368 | tf_op jit(solution)/shard_map/concatenate | solution.py:21
  111.7 6.6 %fusion.41 = (bf16[1,1536,1536]{1,2,0:T(8,128)(2,1)S(1)}, bf16[1,1536,1536]{1,2,0:T(8,128)(2,1)}) fusion(bf16[2,1536,1536]{1,2,0:T(8,128)(2,1)} %pad_maximum_fusion), kind=kLoop, calls=%fused_computation.76 | loop fusion | bytes 18874368 | tf_op jit(solution)/shard_map/slice | solution.py:41
  118.3 6.4 %fusion.30 = f32[4,1536,512]{2,1,0:T(8,128)} fusion(bf16[1536,12,128]{0,2,1:T(8,128)(2,1)S(1)} %bitcast.84, bf16[512,12,128]{0,2,1:T(8,128)(2,1)S(1)} %bitcast.89), kind=kOutput, calls=%fused_computation.52 | convolution fusion | flops 805306368 | bytes 17825792 | tf_op jit(solution)/shard_map/qhd,khd->hqk/dot_general | solution.py:26
  124.7 6.3 %fusion.28 = f32[4,1536,512]{2,1,0:T(8,128)} fusion(bf16[1536,12,128]{0,2,1:T(8,128)(2,1)S(1)} %bitcast.85, bf16[512,12,128]{0,2,1:T(8,128)(2,1)S(1)} %bitcast.90), kind=kOutput, calls=%fused_computation.50 | convolution fusion | flops 805306368 | bytes 17825792 | tf_op jit(solution)/shard_map/qhd,khd->hqk/dot_general | solution.py:26
  131.0 6.3 %fusion.26 = f32[4,1536,512]{2,1,0:T(8,128)} fusion(bf16[1536,12,128]{0,2,1:T(8,128)(2,1)S(1)} %bitcast.86, bf16[512,12,128]{0,2,1:T(8,128)(2,1)S(1)} %bitcast.91), kind=kOutput, calls=%fused_computation.48 | convolution fusion | flops 805306368 | bytes 17825792 | tf_op jit(solution)/shard_map/qhd,khd->hqk/dot_general | solution.py:26
  137.3 14.2 %fusion.44 = (f32[4,512]{1,0:T(4,128)S(1)}, f32[4,512,1536]{1,2,0:T(8,128)}) fusion(f32[4,1536,512]{2,1,0:T(8,128)} %fusion.30, pred[512,1536]{0,1:T(8,128)(4,1)S(1)} %copy-done.5), kind=kOutput, calls=%fused_computation.79 | output fusion | flops 22021632 | bytes 25960448 | tf_op jit(solution)/shard_map/sub | solution.py:31
  151.5 14.5 %fusion.43 = (f32[4,512]{1,0:T(4,128)S(1)}, f32[4,512,1536]{1,2,0:T(8,128)}) fusion(f32[4,1536,512]{2,1,0:T(8,128)} %fusion.28, pred[512,1536]{0,1:T(8,128)(4,1)S(1)} %copy-done.5), kind=kOutput, calls=%fused_computation.78 | output fusion | flops 22021632 | bytes 25960448 | tf_op jit(solution)/shard_map/sub | solution.py:31
  166.0 14.1 %fusion.42 = (f32[4,512]{1,0:T(4,128)S(1)}, f32[4,512,1536]{1,2,0:T(8,128)}) fusion(f32[4,1536,512]{2,1,0:T(8,128)} %fusion.26, pred[512,1536]{0,1:T(8,128)(4,1)S(1)} %copy-done.5), kind=kOutput, calls=%fused_computation.77 | output fusion | flops 22021632 | bytes 25960448 | tf_op jit(solution)/shard_map/sub | solution.py:31
  180.1 5.7 fusion.21
  185.8 5.7 fusion.22
  191.5 5.7 fusion.23
  198.5 41.1 %all-to-all-done.2 = bf16[16,64,3072]{2,1,0:T(8,128)(2,1)} async-done(((bf16[16,64,3072]{2,1,0:T(8,128)(2,1)}), bf16[16,64,3072]{2,1,0:T(8,128)(2,1)}, u32[]{:S(2)}, u32[]{:S(2)}) %all-to-all-start.2) | async-done | bytes 6291488 | tf_op jit(solution)/shard_map/all_to_all | solution.py:110
  239.6 10.0 %gather_fusion.1 = bf16[512,3072]{1,0:T(8,128)(2,1)S(1)} fusion(bf16[1024,3072]{1,0:T(8,128)(2,1)} %bitcast.19, s32[1024]{0:T(1024)S(1)} %pad_clamp_fusion), kind=kCustom, calls=%fused_computation.1 | custom fusion | bytes 6293504 | tf_op jit(solution)/shard_map/gather | solution.py:117
  249.5 10.5 %fusion.45 = f32[1536,3072]{1,0:T(8,128)} fusion(bf16[512,1536]{0,1:T(8,128)(2,1)} %bitcast.97, bf16[512,3072]{1,0:T(8,128)(2,1)S(1)} %gather_fusion.1), kind=kOutput, calls=%fused_computation.80 | convolution fusion | flops 4831838208 | bytes 23592960 | tf_op jit(solution)/shard_map/th,td->hd/dot_general | solution.py:119
  261.5 9.0 %convolution_convert_fusion.1 = bf16[512,3072]{1,0:T(8,128)(2,1)S(1)} fusion(bf16[512,1536]{0,1:T(8,128)(2,1)S(1)} %bitcast.98, bf16[1536,3072]{1,0:T(8,128)(2,1)} %param.13), kind=kOutput, calls=%fused_computation.33 | convolution fusion | flops 4833411072 | bytes 14155776 | tf_op jit(solution)/shard_map/dot_general | solution.py:85
  275.9 6.8 %all-to-all-start.1 = ((bf16[16,64,3072]{2,1,0:T(8,128)(2,1)}), bf16[16,64,3072]{2,1,0:T(8,128)(2,1)}, u32[]{:S(2)}, u32[]{:S(2)}) async-start(bf16[16,64,3072]{2,1,0:T(8,128)(2,1)} %bitcast.88), calls=%async_computation.1 | async-start | bytes 12582912 | tf_op jit(solution)/shard_map/all_to_all | solution.py:94
  283.9 210.3 %all-to-all-done.1 = bf16[16,64,3072]{2,1,0:T(8,128)(2,1)} async-done(((bf16[16,64,3072]{2,1,0:T(8,128)(2,1)}), bf16[16,64,3072]{2,1,0:T(8,128)(2,1)}, u32[]{:S(2)}, u32[]{:S(2)}) %all-to-all-start.1) | async-done | bytes 6291488 | tf_op jit(solution)/shard_map/all_to_all | solution.py:94
  494.2 8.2 %add_convert_fusion = bf16[512,3072]{1,0:T(8,128)(2,1)} fusion(bf16[512,3072]{1,0:T(8,128)(2,1)} %param.14, bf16[1024,3072]{1,0:T(8,128)(2,1)} %bitcast.14, s32[1024]{0:T(1024)S(1)} %eq.78), kind=kOutput, calls=%fused_computation.18 | convolution fusion | flops 3226468352 | bytes 12587008 | tf_op jit(solution)/shard_map/dot_general | solution.py:101
  502.4 64.4 %reduce-scatter.2.cloned.1.call-done = f32[96,3072]{1,0:T(8,128)} async-done(((f32[1536,3072]{1,0:T(8,128)}), f32[96,3072]{1,0:T(8,128)}) %reduce-scatter.2.cloned.1.call-update) | async-done | bytes 1179664 | tf_op jit(solution)/shard_map/reduce_scatter | solution.py:118
  (63 shorter events, 28.0 us)
Async XLA Ops:
  7.2 78.4 %copy-start = (bf16[512,3072]{1,0:T(8,128)(2,1)S(1)}, bf16[512,3072]{1,0:T(8,128)(2,1)}, u32[]{:S(2)}) copy-start(bf16[512,3072]{1,0:T(8,128)(2,1)} %param.15) | copy-start | bytes 9437188
  7.2 11.3 %copy-start.9 = (s32[512,1]{0,1:T(1,128)S(1)}, s32[512,1]{0,1:T(1,128)}, u32[]{:S(2)}) copy-start(s32[512,1]{0,1:T(1,128)} %param.11) | copy-start | bytes 6148
  7.2 12.8 %copy-start.12 = (s32[512]{0:T(512)S(1)}, s32[512]{0:T(512)}, u32[]{:S(2)}) copy-start(s32[512]{0:T(512)} %param.12) | copy-start | bytes 6148
  7.2 19.6 %copy-start.8 = (s32[8192]{0:T(1024)S(1)}, s32[8192]{0:T(1024)}, u32[]{:S(2)}) copy-start(s32[8192]{0:T(1024)} %param.10) | copy-start | bytes 98308
  12.0 92.0 %collective-permute-start = (bf16[2,512,1536]{1,2,0:T(8,128)(2,1)}, bf16[2,512,1536]{1,2,0:T(8,128)(2,1)}, u32[]{:S(2)}, u32[]{:S(2)}) collective-permute-start(bf16[2,512,1536]{1,2,0:T(8,128)(2,1)} %copy.59), channel_id=1, source_target_pairs={{0,1},{1,2},{2,3},{3,4},{4,5},{5,6},{6,7},{7,8},{8,9},{9,10},{10,1... | collective-permute-start | bytes 9437192 | tf_op jit(solution)/shard_map/ppermute | solution.py:19
  13.9 90.1 %collective-permute-start.1 = (bf16[2,512,1536]{1,2,0:T(8,128)(2,1)}, bf16[2,512,1536]{1,2,0:T(8,128)(2,1)}, u32[]{:S(2)}, u32[]{:S(2)}) collective-permute-start(bf16[2,512,1536]{1,2,0:T(8,128)(2,1)} %copy.59), channel_id=1, source_target_pairs={{1,0},{2,1},{3,2},{4,3},{5,4},{6,5},{7,6},{8,7},{9,8},{10,9},{11,1... | collective-permute-start | bytes 9437192 | tf_op jit(solution)/shard_map/ppermute | solution.py:20
  20.0 0.6 copy-start.10
  21.4 64.1 %all-to-all-start = ((s32[16,1,64]{2,1,0:T(1,128)}), s32[16,1,64]{2,1,0:T(1,128)S(1)}, u32[]{:S(2)}, u32[]{:S(2)}) async-start(s32[16,1,64]{2,1,0:T(1,128)} %select_n.56), calls=%async_computation | async-start | bytes 16384 | tf_op jit(solution)/shard_map/all_to_all | solution.py:95
  85.5 6.9 %copy-start.6 = (s32[16,1,64]{2,1,0:T(1,128)}, s32[16,1,64]{2,1,0:T(1,128)S(1)}, u32[]{:S(2)}) copy-start(s32[16,1,64]{2,1,0:T(1,128)S(1)} %all-to-all-done) | copy-start | bytes 12292
  98.2 5.8 %copy-start.2 = (bf16[2,512,1536]{1,2,0:T(8,128)(2,1)S(1)}, bf16[2,512,1536]{1,2,0:T(8,128)(2,1)}, u32[]{:S(2)}) copy-start(bf16[2,512,1536]{1,2,0:T(8,128)(2,1)} %copy.59) | copy-start | bytes 9437188
  98.2 141.4 %all-to-all-start.2 = ((bf16[16,64,3072]{2,1,0:T(8,128)(2,1)}), bf16[16,64,3072]{2,1,0:T(8,128)(2,1)}, u32[]{:S(2)}, u32[]{:S(2)}) async-start(bf16[16,64,3072]{2,1,0:T(8,128)(2,1)} %broadcast_select_fusion), calls=%async_computation.2 | async-start | bytes 12582912 | tf_op jit(solution)/shard_map/all_to_all | solution.py:110
  103.8 463.0 %reduce-scatter.2.cloned.1.call-start = ((), (), s32[]{:S(2)}) async-start(), calls=%async_computation.4 | async-start | bytes 20054016 | tf_op jit(solution)/shard_map/reduce_scatter | solution.py:118
  111.7 6.6 %copy-start.3 = (bf16[512,1536]{0,1:T(8,128)(2,1)S(1)}, bf16[512,1536]{0,1:T(8,128)(2,1)}, u32[]{:S(2)}) copy-start(bf16[512,1536]{0,1:T(8,128)(2,1)} %copy.63) | copy-start | bytes 4718596
  131.0 6.3 %copy-start.5 = (pred[512,1536]{0,1:T(8,128)(4,1)S(1)}, pred[512,1536]{0,1:T(8,128)(4,1)}, u32[]{:S(2)}) copy-start(pred[512,1536]{0,1:T(8,128)(4,1)} %broadcast_compare_fusion) | copy-start | bytes 2359300
  151.5 28.6 %slice-start = ((s8[4718592]{0:T(1024)(128)(4,1)}), s8[4194304]{0:T(1024)(128)(4,1)S(1)}, s32[]{:S(2)}) async-start(s8[4718592]{0:T(1024)(128)(4,1)} %bitcast.92), calls=%async_computation.5 | async-start | bytes 8388608
  166.0 14.1 %slice-start.1 = ((s8[4718592]{0:T(1024)(128)(4,1)}), s8[524288]{0:T(1024)(128)(4,1)S(1)}, s32[]{:S(2)}) async-start(s8[4718592]{0:T(1024)(128)(4,1)} %bitcast.92), calls=%async_computation.6 | async-start | bytes 1048576
  260.0 1.4 copy-start.4
  261.5 9.1 %copy-start.11 = (s32[512]{0:T(512)S(1)}, s32[512]{0:T(512)}, u32[]{:S(2)}) copy-start(s32[512]{0:T(512)} %copy-done.10) | copy-start | bytes 6148
  275.9 7.3 %copy-start.7 = (s32[16,1,64]{2,1,0:T(1,128)S(1)}, s32[16,1,64]{2,1,0:T(1,128)}, u32[]{:S(2)}) copy-start(s32[16,1,64]{2,1,0:T(1,128)} %copy-done.6) | copy-start | bytes 12292
  275.9 218.3 %all-to-all-start.1 = ((bf16[16,64,3072]{2,1,0:T(8,128)(2,1)}), bf16[16,64,3072]{2,1,0:T(8,128)(2,1)}, u32[]{:S(2)}, u32[]{:S(2)}) async-start(bf16[16,64,3072]{2,1,0:T(8,128)(2,1)} %bitcast.88), calls=%async_computation.1 | async-start | bytes 12582912 | tf_op jit(solution)/shard_map/all_to_all | solution.py:94
  494.2 72.6 %copy-start.1 = (bf16[512,3072]{1,0:T(8,128)(2,1)S(1)}, bf16[512,3072]{1,0:T(8,128)(2,1)}, u32[]{:S(2)}) copy-start(bf16[512,3072]{1,0:T(8,128)(2,1)} %param.15) | copy-start | bytes 9437188
Sparse Core Ops, SparseCore 0:
  260.2 306.5 reduce-scatter.1
where the time goes:
time: 581 us; the launch traced here: 574 us
  waiting for transfers between devices  370 us (64%)
  matrix products  69.2 us (12%)
  other arithmetic  61.6 us (11%)
  local copies, waits for them, and re-layouts  33.9 us (6%)
  starting transfers between devices  24.4 us (4%)
  between operations  14.7 us (3%)
    all_to_all x1, waiting for transfers between devices, body(): lax.all_to_all(outgoing, 'seq', split_axis=0, concat_axis=0, tiled=True)  210 us
    reduce_scatter x1, waiting for transfers between devices, body(): lax.psum_scatter(jnp.einsum('th,td->hd', attended, right_rows, preferred_...  64.4 us
    all_to_all x1, waiting for transfers between devices, body(): lax.all_to_all(slot_table, 'seq', split_axis=0, concat_axis=0, tiled=True)  54.5 us
    sub x3, other arithmetic, attend_group(): exp_scores = jnp.where(keep_mask, jnp.exp(scores - row_peak), 0.0)  42.8 us
    all_to_all x1, waiting for transfers between devices, body(): lax.all_to_all(picked.reshape(shard_count, capacity, model_width), 'seq',...  41.1 us
    dot_general x3, matrix products, attend_group(): jnp.einsum('qhd,khd->hqk', query_heads, key_heads, preferred_element_type...  19 us
    dot_general x3, matrix products, attend_group(): jnp.einsum('hqk,khd->qhd', attn_weights, value_heads, preferred_element_t...  17 us
  transfers between devices with their start and end apart: 6, of which 4 were waited for; matrix products, arithmetic and copies ran while one was open for 24% of the time, Pallas kernels for 0%

commit v1 on v0

v1 whole, which is shorter than its diff:
```python
import functools
import math

import jax
import jax.numpy as jnp
from jax import lax
from jax.experimental import pallas as pl
from jax.experimental.pallas import tpu as pltpu
from jax.sharding import PartitionSpec as P

HEAD = 128
SEG_MAX = 512
QUERY_BLOCK = 256
KEY_BLOCK = 256
HEADS_PER_STEP = 3
HEAD_CHUNKS = 1
GRAD_CHUNKS = 2
MASKED = -1e30
EXP2_SCALE = HEAD ** (-0.5) * math.log2(math.e)


def attend_kernel(
    bounds, query_ref, before_ref, own_ref, after_ref, query_seg_ref, key_seg_ref, place_ref,
    out_ref, attended_ref,
):
    row_count = query_ref.shape[0]
    for block in range(row_count // QUERY_BLOCK):
        rows = slice(block * QUERY_BLOCK, (block + 1) * QUERY_BLOCK)
        query_seg = query_seg_ref[:, rows]
        heads = [slice(h * HEAD, (h + 1) * HEAD) for h in range(HEADS_PER_STEP)]
        queries = [query_ref[rows, head] for head in heads]

        def step(pair_ref, first_key, key_block, state):
            offset = pl.multiple_of(key_block * KEY_BLOCK, KEY_BLOCK)
            key_seg = key_seg_ref[pl.ds(first_key + offset, KEY_BLOCK), :]
            keep = key_seg == query_seg
            result = []
            for head, query, (peak, total, summed) in zip(heads, queries, state):
                keys = pair_ref[0, pl.ds(offset, KEY_BLOCK), head]
                values = pair_ref[1, pl.ds(offset, KEY_BLOCK), head]
                scores = lax.dot_general(
                    keys, query, (((1,), (1,)), ((), ())), preferred_element_type=jnp.float32
                )
                scores = jnp.where(keep, scores, MASKED)
                new_peak = jnp.maximum(peak, jnp.max(scores, axis=0, keepdims=True))
                weights = jnp.exp2((scores - new_peak) * EXP2_SCALE)
                shrink = jnp.exp2((peak - new_peak) * EXP2_SCALE)
                total = total * shrink + jnp.sum(weights, axis=0, keepdims=True)
                summed = summed * shrink + lax.dot_general(
                    values,
                    weights.astype(jnp.bfloat16),
                    (((0,), (0,)), ((), ())),
                    preferred_element_type=jnp.float32,
                )
                result.append((new_peak, total, summed))
            return tuple(result)

        state = tuple(
            (
                jnp.full((1, QUERY_BLOCK), MASKED, jnp.float32),
                jnp.zeros((1, QUERY_BLOCK), jnp.float32),
                jnp.zeros((HEAD, QUERY_BLOCK), jnp.float32),
            )
            for _ in heads
        )
        for part, pair_ref in enumerate((before_ref, own_ref, after_ref)):
            first_key = (0, SEG_MAX, SEG_MAX + row_count)[part]
            state = lax.fori_loop(
                bounds[block, 2 * part],
                bounds[block, 2 * part + 1],
                functools.partial(step, pair_ref, first_key),
                state,
            )
        for head, (peak, total, summed) in zip(heads, state):
            attended_ref[rows, head] = (summed * (1.0 / total)).T.astype(jnp.bfloat16)
    out_ref[...] = jnp.dot(
        place_ref[...], attended_ref[...], preferred_element_type=jnp.float32
    ).astype(jnp.bfloat16)


def attend_and_place(queries, first_column, before, own, after, query_seg, key_seg, bounds, placement):
    row_count = queries.shape[0]
    slot_count = placement.shape[0]
    width = before.shape[2]
    step_width = HEADS_PER_STEP * HEAD
    first_step = first_column // step_width
    whole = lambda shape: pl.BlockSpec(shape, lambda i, b: (0,) * len(shape))
    return pl.pallas_call(
        attend_kernel,
        out_shape=jax.ShapeDtypeStruct((slot_count, width), jnp.bfloat16),
        grid_spec=pltpu.PrefetchScalarGridSpec(
            num_scalar_prefetch=1,
            grid=(width // step_width,),
            in_specs=[
                pl.BlockSpec((row_count, step_width), lambda i, b: (0, first_step + i)),
                pl.BlockSpec((2, SEG_MAX, step_width), lambda i, b: (0, 0, i)),
                pl.BlockSpec((2, row_count, step_width), lambda i, b: (0, 0, first_step + i)),
                pl.BlockSpec((2, SEG_MAX, step_width), lambda i, b: (0, 0, i)),
                whole((1, row_count)),
                whole((row_count + 2 * SEG_MAX, 1)),
                whole((slot_count, row_count)),
            ],
            out_specs=pl.BlockSpec((slot_count, step_width), lambda i, b: (0, i)),
            scratch_shapes=[pltpu.VMEM((row_count, step_width), jnp.bfloat16)],
        ),
        compiler_params=pltpu.CompilerParams(vmem_limit_bytes=48 << 20),
        name="attend",
    )(bounds, queries, before, own, after, query_seg, key_seg, placement)


def key_ranges(segment_ids, query_seg, first_row):
    row_count = query_seg.shape[0]
    firsts = query_seg[::QUERY_BLOCK]
    lasts = query_seg[QUERY_BLOCK - 1 :: QUERY_BLOCK]
    low = jnp.sum((segment_ids[None, :] < firsts[:, None]).astype(jnp.int32), axis=1)
    high = jnp.sum((segment_ids[None, :] <= lasts[:, None]).astype(jnp.int32), axis=1)
    columns = []
    for start, length in ((-SEG_MAX, SEG_MAX), (0, row_count), (row_count, SEG_MAX)):
        part_low = jnp.clip(low - first_row - start, 0, length)
        part_high = jnp.clip(high - first_row - start, 0, length)
        columns += [part_low // KEY_BLOCK, (part_high + KEY_BLOCK - 1) // KEY_BLOCK]
    return jnp.stack(columns, axis=1)


def body(
    queries, keys_values, segment_ids, route_shard, route_slot, control_proj, base_hidden, cotangent
):
    row_count = queries.shape[0]
    width = queries.shape[1]
    model_width = control_proj.shape[1]
    shard_count = lax.axis_size("seq")
    shard_index = lax.axis_index("seq")
    capacity = 2 * row_count // shard_count
    slot_count = shard_count * capacity
    block_rows = width // shard_count
    far_count = shard_count // 4

    def swap(value, bit):
        return lax.ppermute(value, "seq", [(i, i ^ bit) for i in range(shard_count)])

    up = [(i, i + 1) for i in range(shard_count - 1)]
    down = [(j, i) for i, j in up]
    chunk_width = width // HEAD_CHUNKS
    halos = []
    for chunk in range(HEAD_CHUNKS):
        columns = slice(chunk * chunk_width, (chunk + 1) * chunk_width)
        before = lax.ppermute(keys_values[:, row_count - SEG_MAX :, columns], "seq", up)
        after = lax.ppermute(keys_values[:, :SEG_MAX, columns], "seq", down)
        halos.append((before, after))
    peer_cotangent = swap(cotangent, 1)

    target_shard = route_shard[:, 0]
    one_hot = (target_shard[:, None] == jnp.arange(shard_count, dtype=jnp.int32)[None, :]).astype(
        jnp.int32
    )
    slot_rank = jnp.sum((jnp.cumsum(one_hot, axis=0) - 1) * one_hot, axis=1)
    flat_place = target_shard * capacity + slot_rank
    place_mask = flat_place[None, :] == jnp.arange(slot_count, dtype=jnp.int32)[:, None]
    placement = place_mask.astype(jnp.bfloat16)
    occupied = jnp.sum(place_mask.astype(jnp.int32), axis=1)
    slot_values = jnp.sum(jnp.where(place_mask, route_slot[None, :], 0), axis=1)
    slot_table = jnp.where(occupied > 0, slot_values, -1).reshape(shard_count, capacity)
    incoming_slots = lax.all_to_all(slot_table, "seq", split_axis=0, concat_axis=0, tiled=True)
    landing = (
        incoming_slots.reshape(-1)[:, None] == jnp.arange(row_count, dtype=jnp.int32)[None, :]
    ).astype(jnp.bfloat16)

    first_row = shard_index * row_count
    query_seg = lax.dynamic_slice_in_dim(segment_ids, first_row, row_count)
    padded_seg = jnp.pad(segment_ids, (SEG_MAX, SEG_MAX), constant_values=-1)
    key_seg = lax.dynamic_slice_in_dim(padded_seg, first_row, row_count + 2 * SEG_MAX)
    bounds = key_ranges(segment_ids, query_seg, first_row)

    landed = []
    for chunk, (before, after) in enumerate(halos):
        outgoing = attend_and_place(
            queries, chunk * chunk_width, before, keys_values, after,
            query_seg[None, :], key_seg[:, None], bounds, placement,
        )
        incoming = lax.all_to_all(
            outgoing.reshape(shard_count, capacity, chunk_width),
            "seq",
            split_axis=0,
            concat_axis=0,
            tiled=True,
        )
        landed.append(
            jnp.einsum(
                "sk,sr->kr",
                incoming.reshape(slot_count, chunk_width),
                landing,
                preferred_element_type=jnp.float32,
            ).astype(jnp.bfloat16)
        )
    landed = jnp.concatenate(landed, axis=0)

    core = shard_index % 2
    near = (shard_index // 2) % 2
    far = shard_index // 4
    by_core = landed.reshape(2 * far_count, 2, block_rows, row_count)
    peer_landed = swap(lax.dynamic_index_in_dim(by_core, 1 - core, 1, keepdims=False), 1)
    own_landed = lax.dynamic_index_in_dim(by_core, core, 1, keepdims=False)
    both_landed = jnp.concatenate([own_landed, peer_landed], axis=2)
    by_near = both_landed.reshape(far_count, 2, block_rows, 2 * row_count)
    sent_rows = lax.dynamic_index_in_dim(by_near, 1 - near, 1, keepdims=False)
    kept_rows = lax.dynamic_index_in_dim(by_near, near, 1, keepdims=False)
    both_cotangent = jnp.concatenate([cotangent, peer_cotangent], axis=0)
    grad_pieces = []
    grad_width = model_width // GRAD_CHUNKS
    for chunk in range(GRAD_CHUNKS):
        columns = slice(chunk * grad_width, (chunk + 1) * grad_width)
        product = lambda rows: jnp.einsum(
            "fbt,td->fbd", rows, both_cotangent[:, columns], preferred_element_type=jnp.float32
        )
        arrived = swap(product(sent_rows).astype(jnp.bfloat16), 2)
        summed = product(kept_rows) + arrived.astype(jnp.float32)
        total = lax.dynamic_index_in_dim(summed, far, 0, keepdims=False)
        rounded = summed.astype(jnp.bfloat16)
        for other in range(1, far_count):
            piece = lax.dynamic_index_in_dim(rounded, far ^ other, 0, keepdims=False)
            total = total + swap(piece, 4 * other).astype(jnp.float32)
        grad_pieces.append(total)
    proj_grad = jnp.concatenate(grad_pieces, axis=1)

    added = jnp.einsum("kr,kd->rd", landed, control_proj, preferred_element_type=jnp.float32)
    mixed_hidden = (base_hidden.astype(jnp.float32) + added).astype(jnp.bfloat16)
    return (mixed_hidden, proj_grad)


def solution(mesh):
    placed = (
        P(("grp", "seq"), None),
        P(None, ("grp", "seq"), None),
        P("grp"),
        P(("grp", "seq"), None),
        P(("grp", "seq")),
        P(),
        P(("grp", "seq"), None),
        P(("grp", "seq"), None),
    )
    return jax.shard_map(
        body,
        mesh=mesh,
        in_specs=placed,
        out_specs=(P(("grp", "seq"), None), P(("grp", "seq"), None)),
        check_vma=False,
    )
```

time: 581 us -> 286 us (0.49)
  waiting for transfers between devices: 370 us -> 149 us
  other arithmetic: 61.6 us -> 8.18 us
  matrix products: 69.2 us -> 16.1 us
  starting transfers between devices: 24.4 us -> 64.6 us
  Pallas kernels: 0 us -> 37.8 us
  local copies, waits for them, and re-layouts: 33.9 us -> 6.74 us
  between operations: 14.7 us -> 0.88 us
    all_to_all x2 -> x1, waiting for transfers between devices: 251 us -> 65.1 us  [body(): lax.all_to_all(outgoing.reshape(shard_count, capacity, chunk_width), 'seq...]
    ppermute x2 -> x12, waiting for transfers between devices: 0.01 us -> 84 us  [the longest x10 64 us: swap(): lax.ppermute(value, 'seq', [(i, i ^ bit) for i in range(shard_count)])]
    reduce_scatter x1 -> x0, waiting for transfers between devices: 64.4 us -> none  [body(): lax.psum_scatter(jnp.einsum('th,td->hd', attended, right_rows, preferred_...]
    all_to_all x1, waiting for transfers between devices: 54.5 us -> 0.01 us  [body(): lax.all_to_all(slot_table, 'seq', split_axis=0, concat_axis=0, tiled=True)]
    dot_general x10 -> x6, matrix products: 69.2 us -> 16.1 us  [the longest x1 6.72 us: body(): jnp.einsum('kr,kd->rd', landed, control_proj, preferred_element_type=jnp....]
    sub x3 -> x1, other arithmetic: 42.8 us -> 0.01 us  [key_ranges(): columns += [part_low // KEY_BLOCK, (part_high + KEY_BLOCK - 1) // KEY_BLOCK]]
    pallas_call x0 -> x1, Pallas kernels: none -> 37.8 us  [attend_and_place(): pl.pallas_call(attend_kernel, out_shape=jax.ShapeDtypeStruct((slot_count,...]
    all_to_all x2 -> x1, starting transfers between devices: 12.4 us -> 39.1 us  [body(): lax.all_to_all(outgoing.reshape(shard_count, capacity, chunk_width), 'seq...]
  transfers between devices with their start and end apart: 6 -> 14, of which waited for: 4 -> 8; matrix products, arithmetic and copies ran while one was open for 24% -> 10% of each run, Pallas kernels for 0% -> 13%
where the time goes in v1:
time: 286 us; the launch traced here: 283 us
  waiting for transfers between devices  149 us (52%)
  starting transfers between devices  64.6 us (23%)
  Pallas kernels  37.8 us (13%)
  matrix products  16.1 us (6%)
  other arithmetic  8.18 us (3%)
  local copies, waits for them, and re-layouts  6.74 us (2%)
    all_to_all x1, waiting for transfers between devices, body(): lax.all_to_all(outgoing.reshape(shard_count, capacity, chunk_width), 'seq...  65.1 us
    ppermute x10, waiting for transfers between devices, swap(): lax.ppermute(value, 'seq', [(i, i ^ bit) for i in range(shard_count)])  64 us
    all_to_all x1, starting transfers between devices, body(): lax.all_to_all(outgoing.reshape(shard_count, capacity, chunk_width), 'seq...  39.1 us
    pallas_call x1, Pallas kernels, attend_and_place(): pl.pallas_call(attend_kernel, out_shape=jax.ShapeDtypeStruct((slot_count,...  37.8 us
    ppermute x1, waiting for transfers between devices, body(): lax.ppermute(keys_values[:, row_count - SEG_MAX:, columns], 'seq', up)  18.3 us
    ppermute x10, starting transfers between devices, swap(): lax.ppermute(value, 'seq', [(i, i ^ bit) for i in range(shard_count)])  13.5 us
    dot_general x1, matrix products, body(): jnp.einsum('kr,kd->rd', landed, control_proj, preferred_element_type=jnp....  6.72 us
  transfers between devices with their start and end apart: 14, of which 8 were waited for; matrix products, arithmetic and copies ran while one was open for 10% of the time, Pallas kernels for 13%

profile of v1, /device:TPU:10, one launch (start us, length us, event | category | flops | bytes accessed | tf_op | source)
XLA Modules:
  0.0 283.5 jit_solution(8456503997667558547)
XLA Ops:
  0.6 2.1 collective-permute-start
  2.7 4.5 %collective-permute-start.1 = (bf16[2,512,1536]{2,1,0:T(8,128)(2,1)}, bf16[2,512,1536]{2,1,0:T(8,128)(2,1)}, u32[]{:S(2)}, u32[]{:S(2)}) collective-permute-start(bf16[2,512,1536]{2,1,0:T(8,128)(2,1)} %own_ref.1), channel_id=1, source_target_pairs={{1,0},{2,1},{3,2},{4,3},{5,4},{6,5},{7,6},{8,7},{9,8},{10,9},{11,1... | collective-permute-start | bytes 9437192 | tf_op jit(solution)/shard_map/ppermute | solution.py:148
  12.8 5.5 %all-to-all-start.1 = ((s32[16,1,64]{2,1,0:T(1,128)}), s32[16,1,64]{2,1,0:T(1,128)S(1)}, u32[]{:S(2)}, u32[]{:S(2)}) async-start(s32[16,1,64]{2,1,0:T(1,128)} %select_n.147), calls=%async_computation.1 | async-start | bytes 16384 | tf_op jit(solution)/shard_map/all_to_all | solution.py:163
  22.5 18.3 %collective-permute-done.before_ref = bf16[2,512,1536]{2,1,0:T(8,128)(2,1)} collective-permute-done((bf16[2,512,1536]{2,1,0:T(8,128)(2,1)}, bf16[2,512,1536]{2,1,0:T(8,128)(2,1)}, u32[]{:S(2)}, u32[]{:S(2)}) %collective-permute-start) | collective-permute-done | bytes 3145760 | tf_op jit(solution)/shard_map/ppermute | solution.py:147
  40.8 1.7 collective-permute-done.1.after_ref
  42.5 37.8 %attend.1 = bf16[1024,1536]{1,0:T(8,128)(2,1)} custom-call(s32[2,6]{1,0:T(2,128)S(1)} %stack.2.bounds, bf16[512,1536]{1,0:T(8,128)(2,1)S(1)} %copy-done, bf16[2,512,1536]{2,1,0:T(8,128)(2,1)} %collective-permute-done.before_ref, bf16[2,512,1536]{2,1,0:T(8,128)(2,1)} %own_ref.1, bf16[2,512,1536]{2,1,0:T(8,128)(2,1)} %collective-permute-done.1.after_ref, ...), custom_call_target="tpu_custom_call" | custom-call | tf_op jit(solution)/shard_map/attend/pallas_call | solution.py:88
  80.3 39.1 %all-to-all-start = ((bf16[16,64,1536]{2,1,0:T(8,128)(2,1)}), bf16[16,64,1536]{2,1,0:T(8,128)(2,1)}, u32[]{:S(2)}, u32[]{:S(2)}) async-start(bf16[16,64,1536]{2,1,0:T(8,128)(2,1)} %bitcast.91), calls=%async_computation | async-start | bytes 6291456 | tf_op jit(solution)/shard_map/all_to_all | solution.py:180
  119.4 1.7 collective-permute-start.3
  122.3 65.1 %all-to-all-done = bf16[16,64,1536]{2,1,0:T(8,128)(2,1)} async-done(((bf16[16,64,1536]{2,1,0:T(8,128)(2,1)}), bf16[16,64,1536]{2,1,0:T(8,128)(2,1)}, u32[]{:S(2)}, u32[]{:S(2)}) %all-to-all-start) | async-done | bytes 3145760 | tf_op jit(solution)/shard_map/all_to_all | solution.py:180
  187.5 3.8 %convolution_convert_fusion = bf16[1536,512]{1,0:T(8,128)(2,1)S(1)} fusion(bf16[1024,1536]{1,0:T(8,128)(2,1)} %bitcast.11, s32[1024]{0:T(1024)S(1)} %eq.64), kind=kOutput, calls=%fused_computation.3 | convolution fusion | flops 1611923456 | bytes 4722688 | tf_op jit(solution)/shard_map/sk,sr->kr/dot_general | solution.py:188
  192.6 2.1 constant_dynamic-update-slice_fusion
  194.7 1.4 convolution_convert_fusion.2
  196.2 1.4 convolution_convert_fusion.1
  197.5 2.7 collective-permute-start.4
  200.3 6.7 %add_convert_fusion = bf16[512,3072]{1,0:T(8,128)(2,1)} fusion(bf16[512,3072]{1,0:T(8,128)(2,1)S(1)} %copy-done.2, bf16[1536,512]{1,0:T(8,128)(2,1)S(1)} %convolution_convert_fusion, bf16[1536,3072]{1,0:T(8,128)(2,1)S(1)} %bitcast.101), kind=kOutput, calls=%fused_computation | convolution fusion | flops 4836556800 | bytes 17301504 | tf_op jit(solution)/shard_map/kr,kd->rd/dot_general | solution.py:225
  207.0 19.9 %collective-permute-done.4 = bf16[4,96,1536]{2,1,0:T(8,128)(2,1)S(1)} collective-permute-done((bf16[4,96,1536]{2,1,0:T(8,128)(2,1)S(1)}, bf16[4,96,1536]{2,1,0:T(8,128)(2,1)S(1)}, u32[]{:S(2)}, u32[]{:S(2)}) %collective-permute-start.4) | collective-permute-done | bytes 1179680 | tf_op jit(solution)/shard_map/ppermute | solution.py:139
  227.0 1.4 fusion.20
  228.5 3.6 %collective-permute-start.6 = (bf16[96,1536]{1,0:T(8,128)(2,1)S(1)}, bf16[96,1536]{1,0:T(8,128)(2,1)S(1)}, u32[]{:S(2)}, u32[]{:S(2)}) collective-permute-start(bf16[96,1536]{1,0:T(8,128)(2,1)S(1)} %get-tuple-element.10), channel_id=1, source_target_pairs={{0,8},{1,9},{2,10},{3,11},{4,12},{5,13},{6,14},{7,15},{8,0},{9,1},... | collective-permute-start | bytes 884744 | tf_op jit(solution)/shard_map/ppermute | solution.py:139
  232.1 19.7 %collective-permute-done.8 = bf16[4,96,1536]{2,1,0:T(8,128)(2,1)S(1)} collective-permute-done((bf16[4,96,1536]{2,1,0:T(8,128)(2,1)S(1)}, bf16[4,96,1536]{2,1,0:T(8,128)(2,1)S(1)}, u32[]{:S(2)}, u32[]{:S(2)}) %collective-permute-start.8) | collective-permute-done | bytes 1179680 | tf_op jit(solution)/shard_map/ppermute | solution.py:139
  253.3 2.5 collective-permute-start.10
  255.8 2.0 collective-permute-start.9
  257.8 12.4 %collective-permute-done.7 = bf16[96,1536]{1,0:T(8,128)(2,1)S(1)} collective-permute-done((bf16[96,1536]{1,0:T(8,128)(2,1)S(1)}, bf16[96,1536]{1,0:T(8,128)(2,1)S(1)}, u32[]{:S(2)}, u32[]{:S(2)}) %collective-permute-start.7) | collective-permute-done | bytes 294944 | tf_op jit(solution)/shard_map/ppermute | solution.py:139
  270.3 6.0 %collective-permute-done.10 = bf16[96,1536]{1,0:T(8,128)(2,1)S(1)} collective-permute-done((bf16[96,1536]{1,0:T(8,128)(2,1)S(1)}, bf16[96,1536]{1,0:T(8,128)(2,1)S(1)}, u32[]{:S(2)}, u32[]{:S(2)}) %collective-permute-start.10) | collective-permute-done | bytes 294944 | tf_op jit(solution)/shard_map/ppermute | solution.py:139
  276.3 6.0 %collective-permute-done.11 = bf16[96,1536]{1,0:T(8,128)(2,1)S(1)} collective-permute-done((bf16[96,1536]{1,0:T(8,128)(2,1)S(1)}, bf16[96,1536]{1,0:T(8,128)(2,1)S(1)}, u32[]{:S(2)}, u32[]{:S(2)}) %collective-permute-start.11) | collective-permute-done | bytes 294944 | tf_op jit(solution)/shard_map/ppermute | solution.py:139
  (64 shorter events, 15.3 us)
Async XLA Ops:
  0.6 41.8 %copy-start = (bf16[512,1536]{1,0:T(8,128)(2,1)S(1)}, bf16[512,1536]{1,0:T(8,128)(2,1)}, u32[]{:S(2)}) copy-start(bf16[512,1536]{1,0:T(8,128)(2,1)} %query_ref.1) | copy-start | bytes 4718596
  0.6 40.1 %collective-permute-start = (bf16[2,512,1536]{2,1,0:T(8,128)(2,1)}, bf16[2,512,1536]{2,1,0:T(8,128)(2,1)}, u32[]{:S(2)}, u32[]{:S(2)}) collective-permute-start(bf16[2,512,1536]{2,1,0:T(8,128)(2,1)} %own_ref.1), channel_id=1, source_target_pairs={{0,1},{1,2},{2,3},{3,4},{4,5},{5,6},{6,7},{7,8},{8,9},{9,10},{10,1... | collective-permute-start | bytes 9437192 | tf_op jit(solution)/shard_map/ppermute | solution.py:147
  2.7 39.7 %collective-permute-start.1 = (bf16[2,512,1536]{2,1,0:T(8,128)(2,1)}, bf16[2,512,1536]{2,1,0:T(8,128)(2,1)}, u32[]{:S(2)}, u32[]{:S(2)}) collective-permute-start(bf16[2,512,1536]{2,1,0:T(8,128)(2,1)} %own_ref.1), channel_id=1, source_target_pairs={{1,0},{2,1},{3,2},{4,3},{5,4},{6,5},{7,6},{8,7},{9,8},{10,9},{11,1... | collective-permute-start | bytes 9437192 | tf_op jit(solution)/shard_map/ppermute | solution.py:148
  12.8 67.5 %all-to-all-start.1 = ((s32[16,1,64]{2,1,0:T(1,128)}), s32[16,1,64]{2,1,0:T(1,128)S(1)}, u32[]{:S(2)}, u32[]{:S(2)}) async-start(s32[16,1,64]{2,1,0:T(1,128)} %select_n.147), calls=%async_computation.1 | async-start | bytes 16384 | tf_op jit(solution)/shard_map/all_to_all | solution.py:163
  80.3 39.1 %copy-start.1 = (bf16[512,3072]{1,0:T(8,128)(2,1)S(1)}, bf16[512,3072]{1,0:T(8,128)(2,1)}, u32[]{:S(2)}) copy-start(bf16[512,3072]{1,0:T(8,128)(2,1)} %param.15) | copy-start | bytes 9437188
  80.3 107.2 %all-to-all-start = ((bf16[16,64,1536]{2,1,0:T(8,128)(2,1)}), bf16[16,64,1536]{2,1,0:T(8,128)(2,1)}, u32[]{:S(2)}, u32[]{:S(2)}) async-start(bf16[16,64,1536]{2,1,0:T(8,128)(2,1)} %bitcast.91), calls=%async_computation | async-start | bytes 6291456 | tf_op jit(solution)/shard_map/all_to_all | solution.py:180
  119.4 73.2 %collective-permute-start.3 = (bf16[512,3072]{1,0:T(8,128)(2,1)S(1)}, bf16[512,3072]{1,0:T(8,128)(2,1)}, u32[]{:S(2)}, u32[]{:S(2)}) collective-permute-start(bf16[512,3072]{1,0:T(8,128)(2,1)S(1)} %copy-done.1), channel_id=1, source_target_pairs={{0,1},{1,0},{2,3},{3,2},{4,5},{5,4},{6,7},{7,6},{8,9},{9,8},{10,11... | collective-permute-start | bytes 9437192 | tf_op jit(solution)/shard_map/ppermute | solution.py:139
  191.4 3.3 %collective-permute-start.2 = (bf16[8,96,512]{2,1,0:T(8,128)(2,1)S(1)}, bf16[8,96,512]{2,1,0:T(8,128)(2,1)S(1)}, u32[]{:S(2)}, u32[]{:S(2)}) collective-permute-start(bf16[8,96,512]{2,1,0:T(8,128)(2,1)S(1)} %get-tuple-element.6), channel_id=1, source_target_pairs={{0,1},{1,0},{2,3},{3,2},{4,5},{5,4},{6,7},{7,6},{8,9},{9,8},{10,11... | collective-permute-start | bytes 2359304 | tf_op jit(solution)/shard_map/ppermute | solution.py:139
  194.7 5.6 %slice-start = ((s8[9437184]{0:T(1024)(128)(4,1)}), s8[4194304]{0:T(1024)(128)(4,1)S(1)}, s32[]{:S(2)}) async-start(s8[9437184]{0:T(1024)(128)(4,1)} %bitcast.100), calls=%async_computation.2 | async-start | bytes 8388608
  194.7 5.6 %slice-start.1 = ((s8[9437184]{0:T(1024)(128)(4,1)}), s8[4194304]{0:T(1024)(128)(4,1)S(1)}, s32[]{:S(2)}) async-start(s8[9437184]{0:T(1024)(128)(4,1)} %bitcast.100), calls=%async_computation.3 | async-start | bytes 8388608
  196.1 4.2 %slice-start.2 = ((s8[9437184]{0:T(1024)(128)(4,1)}), s8[1048576]{0:T(1024)(128)(4,1)S(1)}, s32[]{:S(2)}) async-start(s8[9437184]{0:T(1024)(128)(4,1)} %bitcast.100), calls=%async_computation.4 | async-start | bytes 2097152
  196.1 4.2 %copy-start.2 = (bf16[512,3072]{1,0:T(8,128)(2,1)S(1)}, bf16[512,3072]{1,0:T(8,128)(2,1)}, u32[]{:S(2)}) copy-start(bf16[512,3072]{1,0:T(8,128)(2,1)} %param.14) | copy-start | bytes 9437188
  197.5 29.4 %collective-permute-start.4 = (bf16[4,96,1536]{2,1,0:T(8,128)(2,1)S(1)}, bf16[4,96,1536]{2,1,0:T(8,128)(2,1)S(1)}, u32[]{:S(2)}, u32[]{:S(2)}) collective-permute-start(bf16[4,96,1536]{2,1,0:T(8,128)(2,1)S(1)} %convolution_convert_fusion.2), channel_id=1, source_target_pairs={{0,2},{1,3},{2,0},{3,1},{4,6},{5,7},{6,4},{7,5},{8,10},{9,11},{10,... | collective-permute-start | bytes 3538952 | tf_op jit(solution)/shard_map/ppermute | solution.py:139
  200.2 51.6 %collective-permute-start.8 = (bf16[4,96,1536]{2,1,0:T(8,128)(2,1)S(1)}, bf16[4,96,1536]{2,1,0:T(8,128)(2,1)S(1)}, u32[]{:S(2)}, u32[]{:S(2)}) collective-permute-start(bf16[4,96,1536]{2,1,0:T(8,128)(2,1)S(1)} %convolution_convert_fusion.1), channel_id=1, source_target_pairs={{0,2},{1,3},{2,0},{3,1},{4,6},{5,7},{6,4},{7,5},{8,10},{9,11},{10,... | collective-permute-start | bytes 3538952 | tf_op jit(solution)/shard_map/ppermute | solution.py:139
  228.4 27.4 %collective-permute-start.5 = (bf16[96,1536]{1,0:T(8,128)(2,1)S(1)}, bf16[96,1536]{1,0:T(8,128)(2,1)S(1)}, u32[]{:S(2)}, u32[]{:S(2)}) collective-permute-start(bf16[96,1536]{1,0:T(8,128)(2,1)S(1)} %get-tuple-element.8), channel_id=1, source_target_pairs={{0,4},{1,5},{2,6},{3,7},{4,0},{5,1},{6,2},{7,3},{8,12},{9,13},{10,... | collective-permute-start | bytes 884744 | tf_op jit(solution)/shard_map/ppermute | solution.py:139
  228.5 29.2 %collective-permute-start.6 = (bf16[96,1536]{1,0:T(8,128)(2,1)S(1)}, bf16[96,1536]{1,0:T(8,128)(2,1)S(1)}, u32[]{:S(2)}, u32[]{:S(2)}) collective-permute-start(bf16[96,1536]{1,0:T(8,128)(2,1)S(1)} %get-tuple-element.10), channel_id=1, source_target_pairs={{0,8},{1,9},{2,10},{3,11},{4,12},{5,13},{6,14},{7,15},{8,0},{9,1},... | collective-permute-start | bytes 884744 | tf_op jit(solution)/shard_map/ppermute | solution.py:139
  232.1 38.1 %collective-permute-start.7 = (bf16[96,1536]{1,0:T(8,128)(2,1)S(1)}, bf16[96,1536]{1,0:T(8,128)(2,1)S(1)}, u32[]{:S(2)}, u32[]{:S(2)}) collective-permute-start(bf16[96,1536]{1,0:T(8,128)(2,1)S(1)} %get-tuple-element.9), channel_id=1, source_target_pairs={{0,12},{1,13},{2,14},{3,15},{4,8},{5,9},{6,10},{7,11},{8,4},{9,5},... | collective-permute-start | bytes 884744 | tf_op jit(solution)/shard_map/ppermute | solution.py:139
  253.3 23.0 %collective-permute-start.10 = (bf16[96,1536]{1,0:T(8,128)(2,1)S(1)}, bf16[96,1536]{1,0:T(8,128)(2,1)S(1)}, u32[]{:S(2)}, u32[]{:S(2)}) collective-permute-start(bf16[96,1536]{1,0:T(8,128)(2,1)S(1)} %get-tuple-element.13), channel_id=1, source_target_pairs={{0,8},{1,9},{2,10},{3,11},{4,12},{5,13},{6,14},{7,15},{8,0},{9,1},... | collective-permute-start | bytes 884744 | tf_op jit(solution)/shard_map/ppermute | solution.py:139
  255.8 26.4 %collective-permute-start.11 = (bf16[96,1536]{1,0:T(8,128)(2,1)S(1)}, bf16[96,1536]{1,0:T(8,128)(2,1)S(1)}, u32[]{:S(2)}, u32[]{:S(2)}) collective-permute-start(bf16[96,1536]{1,0:T(8,128)(2,1)S(1)} %get-tuple-element.12), channel_id=1, source_target_pairs={{0,12},{1,13},{2,14},{3,15},{4,8},{5,9},{6,10},{7,11},{8,4},{9,5},... | collective-permute-start | bytes 884744 | tf_op jit(solution)/shard_map/ppermute | solution.py:139
  255.8 26.4 %collective-permute-start.9 = (bf16[96,1536]{1,0:T(8,128)(2,1)S(1)}, bf16[96,1536]{1,0:T(8,128)(2,1)S(1)}, u32[]{:S(2)}, u32[]{:S(2)}) collective-permute-start(bf16[96,1536]{1,0:T(8,128)(2,1)S(1)} %get-tuple-element.11), channel_id=1, source_target_pairs={{0,4},{1,5},{2,6},{3,7},{4,0},{5,1},{6,2},{7,3},{8,12},{9,13},{10,... | collective-permute-start | bytes 884744 | tf_op jit(solution)/shard_map/ppermute | solution.py:139

commit v2 on v1

v2 whole, which is shorter than its diff:
```python
import functools
import math

import jax
import jax.numpy as jnp
from jax import lax
from jax.experimental import pallas as pl
from jax.experimental.pallas import tpu as pltpu
from jax.sharding import PartitionSpec as P

HEAD = 128
SEG_MAX = 512
LOCAL_QUERY_BLOCK = 256
HALO_QUERY_BLOCK = 128
KEY_BLOCK = 256
HEADS_PER_STEP = 3
STEP_WIDTH = HEADS_PER_STEP * HEAD
OUTER_PARTS = 2
INNER_PARTS = 2
LOCAL_FLOPS_HINT = 1 << 33
HALO_FLOPS_HINT = 1 << 34
MASKED = -1e30
EXP2_SCALE = HEAD ** (-0.5) * math.log2(math.e)
HEAD_SLICES = [slice(h * HEAD, (h + 1) * HEAD) for h in range(HEADS_PER_STEP)]


def attend_step(pair_ref, key_seg_ref, query_seg, queries, key_block, state):
    offset = pl.multiple_of(key_block * KEY_BLOCK, KEY_BLOCK)
    keep = key_seg_ref[pl.ds(offset, KEY_BLOCK), :] == query_seg
    result = []
    for head, query, (peak, total, summed) in zip(HEAD_SLICES, queries, state):
        keys = pair_ref[0, pl.ds(offset, KEY_BLOCK), head]
        values = pair_ref[1, pl.ds(offset, KEY_BLOCK), head]
        scores = lax.dot_general(
            keys, query, (((1,), (1,)), ((), ())), preferred_element_type=jnp.float32
        )
        scores = jnp.where(keep, scores, MASKED)
        new_peak = jnp.maximum(peak, jnp.max(scores, axis=0, keepdims=True))
        weights = jnp.exp2((scores - new_peak) * EXP2_SCALE)
        shrink = jnp.exp2((peak - new_peak) * EXP2_SCALE)
        total = total * shrink + jnp.sum(weights, axis=0, keepdims=True)
        summed = summed * shrink + lax.dot_general(
            values,
            weights.astype(jnp.bfloat16),
            (((0,), (0,)), ((), ())),
            preferred_element_type=jnp.float32,
        )
        result.append((new_peak, total, summed))
    return tuple(result)


def local_kernel(bounds, query_ref, own_ref, query_seg_ref, key_seg_ref, summed_ref, stats_ref):
    row_count = query_ref.shape[0]
    for block in range(row_count // LOCAL_QUERY_BLOCK):
        rows = slice(block * LOCAL_QUERY_BLOCK, (block + 1) * LOCAL_QUERY_BLOCK)
        state = tuple(
            (
                jnp.full((1, LOCAL_QUERY_BLOCK), MASKED, jnp.float32),
                jnp.zeros((1, LOCAL_QUERY_BLOCK), jnp.float32),
                jnp.zeros((HEAD, LOCAL_QUERY_BLOCK), jnp.float32),
            )
            for _ in HEAD_SLICES
        )
        state = lax.fori_loop(
            bounds[block, 2],
            bounds[block, 3],
            functools.partial(
                attend_step,
                own_ref,
                key_seg_ref,
                query_seg_ref[:, rows],
                [query_ref[rows, head] for head in HEAD_SLICES],
            ),
            state,
        )
        for h, (peak, total, summed) in enumerate(state):
            stats_ref[0, h : h + 1, rows] = peak
            stats_ref[0, HEADS_PER_STEP + h : HEADS_PER_STEP + h + 1, rows] = total
            summed_ref[HEAD_SLICES[h], rows] = summed


def halo_kernel(
    bounds, query_ref, before_ref, after_ref, query_seg_ref, before_seg_ref, after_seg_ref,
    summed_ref, stats_ref, place_ref, out_ref, attended_ref,
):
    row_count = query_ref.shape[0]
    for block in range(row_count // HALO_QUERY_BLOCK):
        rows = slice(block * HALO_QUERY_BLOCK, (block + 1) * HALO_QUERY_BLOCK)
        queries = [query_ref[rows, head] for head in HEAD_SLICES]
        query_seg = query_seg_ref[:, rows]
        state = tuple(
            (
                stats_ref[0, h : h + 1, rows],
                stats_ref[0, HEADS_PER_STEP + h : HEADS_PER_STEP + h + 1, rows],
                summed_ref[head, rows],
            )
            for h, head in enumerate(HEAD_SLICES)
        )
        for column, pair_ref, seg_ref in ((0, before_ref, before_seg_ref), (4, after_ref, after_seg_ref)):
            state = lax.fori_loop(
                bounds[block, column],
                bounds[block, column + 1],
                functools.partial(attend_step, pair_ref, seg_ref, query_seg, queries),
                state,
            )
        for head, (peak, total, summed) in zip(HEAD_SLICES, state):
            attended_ref[rows, head] = (summed * (1.0 / total)).T.astype(jnp.bfloat16)
    out_ref[...] = jnp.dot(
        place_ref[...], attended_ref[...], preferred_element_type=jnp.float32
    ).astype(jnp.bfloat16)


def whole(*shape):
    return pl.BlockSpec(shape, lambda i, b: (0,) * len(shape))


def step_column(steps):
    return lambda i, b: (0, steps[0] + steps[1] * i)


def step_pair(steps):
    return lambda i, b: (0, 0, steps[0] + steps[1] * i)


def attend_local(queries, pairs, steps, query_seg, bounds):
    row_count = queries.shape[0]
    width = 2 * STEP_WIDTH
    return pl.pallas_call(
        local_kernel,
        out_shape=(
            jax.ShapeDtypeStruct((width, row_count), jnp.float32),
            jax.ShapeDtypeStruct((2, 2 * HEADS_PER_STEP, row_count), jnp.float32),
        ),
        grid_spec=pltpu.PrefetchScalarGridSpec(
            num_scalar_prefetch=1,
            grid=(2,),
            in_specs=[
                pl.BlockSpec((row_count, STEP_WIDTH), step_column(steps)),
                pl.BlockSpec((2, row_count, STEP_WIDTH), step_pair(steps)),
                whole(1, row_count),
                whole(row_count, 1),
            ],
            out_specs=[
                pl.BlockSpec((STEP_WIDTH, row_count), lambda i, b: (i, 0)),
                pl.BlockSpec((1, 2 * HEADS_PER_STEP, row_count), lambda i, b: (i, 0, 0)),
            ],
        ),
        compiler_params=pltpu.CompilerParams(vmem_limit_bytes=48 << 20),
        cost_estimate=pl.CostEstimate(
            flops=LOCAL_FLOPS_HINT, transcendentals=1 << 20, bytes_accessed=1 << 22
        ),
        name="attend_local",
    )(bounds, queries, pairs, query_seg[None, :], query_seg[:, None])


def attend_halo(queries, halo, steps, query_seg, margin_seg, bounds, local, placement):
    row_count = queries.shape[0]
    slot_count = placement.shape[0]
    before, after = halo
    return pl.pallas_call(
        halo_kernel,
        out_shape=jax.ShapeDtypeStruct((slot_count, 2 * STEP_WIDTH), jnp.bfloat16),
        grid_spec=pltpu.PrefetchScalarGridSpec(
            num_scalar_prefetch=1,
            grid=(2,),
            in_specs=[
                pl.BlockSpec((row_count, STEP_WIDTH), step_column(steps)),
                pl.BlockSpec((2, SEG_MAX, STEP_WIDTH), step_pair((0, 1))),
                pl.BlockSpec((2, SEG_MAX, STEP_WIDTH), step_pair((0, 1))),
                whole(1, row_count),
                whole(SEG_MAX, 1),
                whole(SEG_MAX, 1),
                pl.BlockSpec((STEP_WIDTH, row_count), lambda i, b: (i, 0)),
                pl.BlockSpec((1, 2 * HEADS_PER_STEP, row_count), lambda i, b: (i, 0, 0)),
                whole(slot_count, row_count),
            ],
            out_specs=pl.BlockSpec((slot_count, STEP_WIDTH), step_column((0, 1))),
            scratch_shapes=[pltpu.VMEM((row_count, STEP_WIDTH), jnp.bfloat16)],
        ),
        compiler_params=pltpu.CompilerParams(vmem_limit_bytes=48 << 20),
        cost_estimate=pl.CostEstimate(
            flops=HALO_FLOPS_HINT, transcendentals=1 << 20, bytes_accessed=1 << 22
        ),
        name="attend_halo",
    )(
        bounds, queries, before, after, query_seg[None, :],
        margin_seg[:SEG_MAX, None], margin_seg[SEG_MAX + row_count :, None], *local, placement,
    )


def key_ranges(segment_ids, query_seg, first_row, query_block):
    row_count = query_seg.shape[0]
    firsts = query_seg[::query_block]
    lasts = query_seg[query_block - 1 :: query_block]
    low = jnp.sum((segment_ids[None, :] < firsts[:, None]).astype(jnp.int32), axis=1)
    high = jnp.sum((segment_ids[None, :] <= lasts[:, None]).astype(jnp.int32), axis=1)
    columns = []
    for start, length in ((-SEG_MAX, SEG_MAX), (0, row_count), (row_count, SEG_MAX)):
        part_low = jnp.clip(low - first_row - start, 0, length)
        part_high = jnp.clip(high - first_row - start, 0, length)
        columns += [part_low // KEY_BLOCK, (part_high + KEY_BLOCK - 1) // KEY_BLOCK]
    return jnp.stack(columns, axis=1)


def body(
    queries, keys_values, segment_ids, route_shard, route_slot, control_proj, base_hidden, cotangent
):
    row_count = queries.shape[0]
    width = queries.shape[1]
    model_width = control_proj.shape[1]
    shard_count = lax.axis_size("seq")
    shard_index = lax.axis_index("seq")
    capacity = 2 * row_count // shard_count
    slot_count = shard_count * capacity
    block_rows = width // shard_count
    far_count = shard_count // 4
    core = shard_index % 2
    near = (shard_index // 2) % 2
    far = shard_index // 4
    quarter = width // 4
    far_quarter = far_count // 4

    def swap(value, bit):
        return lax.ppermute(value, "seq", [(i, i ^ bit) for i in range(shard_count)])

    def outer(value):
        return jnp.concatenate([value[..., :quarter], value[..., 3 * quarter :]], axis=-1)

    def inner(value):
        return value[..., quarter : 3 * quarter]

    up = [(i, i + 1) for i in range(shard_count - 1)]
    down = [(j, i) for i, j in up]

    def halo(pairs):
        before = lax.ppermute(pairs[:, row_count - SEG_MAX :], "seq", up)
        after = lax.ppermute(pairs[:, :SEG_MAX], "seq", down)
        return before, after

    first_halo = halo(outer(keys_values))
    gated, first_halo = lax.optimization_barrier((inner(keys_values), first_halo))
    second_halo = halo(gated)
    peer_cotangent = swap(cotangent, 1)

    target_shard = route_shard[:, 0]
    one_hot = (target_shard[:, None] == jnp.arange(shard_count, dtype=jnp.int32)[None, :]).astype(
        jnp.int32
    )
    slot_rank = jnp.sum((jnp.cumsum(one_hot, axis=0) - 1) * one_hot, axis=1)
    flat_place = target_shard * capacity + slot_rank
    place_mask = flat_place[None, :] == jnp.arange(slot_count, dtype=jnp.int32)[:, None]
    placement = place_mask.astype(jnp.bfloat16)
    occupied = jnp.sum(place_mask.astype(jnp.int32), axis=1)
    slot_values = jnp.sum(jnp.where(place_mask, route_slot[None, :], 0), axis=1)
    slot_table = jnp.where(occupied > 0, slot_values, -1).reshape(shard_count, capacity)
    incoming_slots = lax.all_to_all(slot_table, "seq", split_axis=0, concat_axis=0, tiled=True)
    landing = (
        incoming_slots.reshape(-1)[:, None] == jnp.arange(row_count, dtype=jnp.int32)[None, :]
    ).astype(jnp.bfloat16)

    first_row = shard_index * row_count
    query_seg = lax.dynamic_slice_in_dim(segment_ids, first_row, row_count)
    padded_seg = jnp.pad(segment_ids, (SEG_MAX, SEG_MAX), constant_values=-1)
    key_seg = lax.dynamic_slice_in_dim(padded_seg, first_row, row_count + 2 * SEG_MAX)
    local_bounds = key_ranges(segment_ids, query_seg, first_row, LOCAL_QUERY_BLOCK)
    halo_bounds = key_ranges(segment_ids, query_seg, first_row, HALO_QUERY_BLOCK)
    head_steps = ((0, 3), (1, 1))
    outer_local = attend_local(queries, keys_values, head_steps[0], query_seg, local_bounds)
    inner_local = attend_local(queries, keys_values, head_steps[1], query_seg, local_bounds)
    outer_local, inner_local, first_halo = lax.optimization_barrier(
        (outer_local, inner_local, first_halo)
    )
    outer_placed = attend_halo(
        queries, first_halo, head_steps[0], query_seg, key_seg, halo_bounds, outer_local, placement
    )
    inner_placed = attend_halo(
        queries, second_halo, head_steps[1], query_seg, key_seg, halo_bounds, inner_local, placement
    )

    def split_columns(parts):
        step = model_width // parts
        return [slice(part * step, (part + 1) * step) for part in range(parts)]

    def product(halves, columns):
        return sum(
            jnp.einsum("fbt,td->fbd", half, other[:, columns], preferred_element_type=jnp.float32)
            for half, other in zip(halves, (cotangent, peer_cotangent))
        )

    def land(value):
        incoming = lax.all_to_all(
            value.reshape(shard_count, capacity, 2 * quarter),
            "seq",
            split_axis=0,
            concat_axis=0,
            tiled=True,
        )
        return jnp.einsum(
            "sk,sr->kr",
            incoming.reshape(slot_count, 2 * quarter),
            landing,
            preferred_element_type=jnp.float32,
        ).astype(jnp.bfloat16)

    def near_reduce(rows, parts):
        by_core = rows.reshape(far_count, 2, block_rows, row_count)
        peer_rows = swap(lax.dynamic_index_in_dim(by_core, 1 - core, 1, keepdims=False), 1)
        own_rows = lax.dynamic_index_in_dim(by_core, core, 1, keepdims=False)
        by_near = [
            value.reshape(far_count // 2, 2, block_rows, row_count) for value in (own_rows, peer_rows)
        ]
        sent_rows = [lax.dynamic_index_in_dim(v, 1 - near, 1, keepdims=False) for v in by_near]
        kept_rows = [lax.dynamic_index_in_dim(v, near, 1, keepdims=False) for v in by_near]
        sent = [product(sent_rows, columns).astype(jnp.bfloat16) for columns in split_columns(parts)]
        summed = [
            product(kept_rows, columns) + swap(value, 2).astype(jnp.float32)
            for columns, value in zip(split_columns(parts), sent)
        ]
        return sent, summed

    def far_exchange(chunk, summed):
        members = [
            f for f in range(far_count) if (far_quarter <= f < 3 * far_quarter) == (chunk == 1)
        ]

        def place_of(index):
            if chunk == 1:
                return index - far_quarter
            return jnp.where(index < far_quarter, index, index - 2 * far_quarter)

        kept = lax.dynamic_index_in_dim(summed, place_of(far), 0, keepdims=False)
        rounded = summed.astype(jnp.bfloat16)
        arrived = []
        for other in range(1, far_count):
            piece = lax.dynamic_index_in_dim(rounded, place_of(far ^ other), 0, keepdims=False)
            routes = [
                (i, i ^ (4 * other)) for i in range(shard_count) if (i // 4) ^ other in members
            ]
            arrived.append(lax.ppermute(piece, "seq", routes))
        return kept, arrived

    def far_total(kept, arrived):
        return kept + sum(value.astype(jnp.float32) for value in arrived)

    outer_rows = land(outer_placed)
    _, outer_summed = near_reduce(outer_rows, OUTER_PARTS)
    outer_far = [far_exchange(0, value) for value in outer_summed]
    inner_rows = land(inner_placed)
    _, inner_summed = near_reduce(inner_rows, INNER_PARTS)
    outer_far, late_rows, inner_summed[0] = lax.optimization_barrier(
        (outer_far, inner_rows, inner_summed[0])
    )
    inner_far = [far_exchange(1, value) for value in inner_summed]
    grad_parts = [
        jnp.concatenate([far_total(*pair) for pair in pairs], axis=1)
        for pairs in (outer_far, inner_far)
    ]
    in_middle = (far >= far_quarter) & (far < 3 * far_quarter)
    proj_grad = jnp.where(in_middle, grad_parts[1], grad_parts[0])

    added = jnp.einsum(
        "kr,kd->rd",
        jnp.concatenate([outer_rows[:quarter], late_rows, outer_rows[quarter:]], axis=0),
        control_proj,
        preferred_element_type=jnp.float32,
    )
    mixed_hidden = (base_hidden.astype(jnp.float32) + added).astype(jnp.bfloat16)
    return (mixed_hidden, proj_grad)


def solution(mesh):
    placed = (
        P(("grp", "seq"), None),
        P(None, ("grp", "seq"), None),
        P("grp"),
        P(("grp", "seq"), None),
        P(("grp", "seq")),
        P(),
        P(("grp", "seq"), None),
        P(("grp", "seq"), None),
    )
    return jax.shard_map(
        body,
        mesh=mesh,
        in_specs=placed,
        out_specs=(P(("grp", "seq"), None), P(("grp", "seq"), None)),
        check_vma=False,
    )
```

time: 286 us -> 236 us (0.83)
  waiting for transfers between devices: 149 us -> 64.6 us
  matrix products: 16.1 us -> 31.4 us
  Pallas kernels: 37.8 us -> 47.9 us
  local copies, waits for them, and re-layouts: 6.74 us -> 13.2 us
  starting transfers between devices: 64.6 us -> 68 us
    all_to_all x1 -> x2, waiting for transfers between devices: 65.1 us -> 20.2 us  [land(): lax.all_to_all(value.reshape(shard_count, capacity, 2 * quarter), 'seq',...]
    ppermute x2 -> x16, starting transfers between devices: 6.6 us -> 38.2 us  [the longest x12 25.3 us: far_exchange(): arrived.append(lax.ppermute(piece, 'seq', routes))]
    ppermute x10 -> x7, waiting for transfers between devices: 64 us -> 37 us  [swap(): lax.ppermute(value, 'seq', [(i, i ^ bit) for i in range(shard_count)])]
    all_to_all x1 -> x2, starting transfers between devices: 39.1 us -> 17.8 us  [land(): lax.all_to_all(value.reshape(shard_count, capacity, 2 * quarter), 'seq',...]
    dot_general x6 -> x19, matrix products: 16.1 us -> 31.4 us  [the longest x16 19.3 us: product(): jnp.einsum('fbt,td->fbd', half, other[:, columns], preferred_element_type...]
    ppermute x2 -> x16, waiting for transfers between devices: 20 us -> 7.41 us  [the longest x12 7.4 us: far_exchange(): arrived.append(lax.ppermute(piece, 'seq', routes))]
    pallas_call x1 -> x4, Pallas kernels: 37.8 us -> 47.9 us  [the longest x2 26.7 us: attend_halo(): pl.pallas_call(halo_kernel, out_shape=jax.ShapeDtypeStruct((slot_count, 2...]
    ppermute x10 -> x7, starting transfers between devices: 13.5 us -> 6.71 us  [swap(): lax.ppermute(value, 'seq', [(i, i ^ bit) for i in range(shard_count)])]
  transfers between devices with their start and end apart: 14 -> 26, of which waited for: 8 -> 8; matrix products, arithmetic and copies ran while one was open for 10% -> 20% of each run, Pallas kernels for 13% -> 20%
where the time goes in v2:
time: 236 us; the launch traced here: 235 us
  starting transfers between devices  68 us (29%)
  waiting for transfers between devices  64.6 us (27%)
  Pallas kernels  47.9 us (20%)
  matrix products  31.4 us (13%)
  local copies, waits for them, and re-layouts  13.2 us (6%)
  other arithmetic  8.78 us (4%)
    ppermute x7, waiting for transfers between devices, swap(): lax.ppermute(value, 'seq', [(i, i ^ bit) for i in range(shard_count)])  37 us
    pallas_call x2, Pallas kernels, attend_halo(): pl.pallas_call(halo_kernel, out_shape=jax.ShapeDtypeStruct((slot_count, 2...  26.7 us
    ppermute x12, starting transfers between devices, far_exchange(): arrived.append(lax.ppermute(piece, 'seq', routes))  25.3 us
    pallas_call x2, Pallas kernels, attend_local(): pl.pallas_call(local_kernel, out_shape=(jax.ShapeDtypeStruct((width, row_...  21.2 us
    all_to_all x2, waiting for transfers between devices, land(): lax.all_to_all(value.reshape(shard_count, capacity, 2 * quarter), 'seq',...  20.2 us
    dot_general x16, matrix products, product(): jnp.einsum('fbt,td->fbd', half, other[:, columns], preferred_element_type...  19.3 us
    all_to_all x2, starting transfers between devices, land(): lax.all_to_all(value.reshape(shard_count, capacity, 2 * quarter), 'seq',...  17.8 us
    ppermute x2, starting transfers between devices, halo(): after = lax.ppermute(pairs[:, :SEG_MAX], 'seq', down)  8.95 us
  transfers between devices with their start and end apart: 26, of which 8 were waited for; matrix products, arithmetic and copies ran while one was open for 20% of the time, Pallas kernels for 20%

profile of v2, /device:TPU:10, one launch (start us, length us, event | category | flops | bytes accessed | tf_op | source)
XLA Modules:
  0.0 235.3 jit_solution(8461886104347547478)
XLA Ops:
  5.4 4.5 %collective-permute-start.1 = (bf16[2,512,768]{2,1,0:T(8,128)(2,1)}, bf16[2,512,768]{2,1,0:T(8,128)(2,1)}, u32[]{:S(2)}, u32[]{:S(2)}) collective-permute-start(bf16[2,512,768]{2,1,0:T(8,128)(2,1)} %pad_maximum_fusion), channel_id=1, source_target_pairs={{1,0},{2,1},{3,2},{4,3},{5,4},{6,5},{7,6},{8,7},{9,8},{10,9},{11,1... | collective-permute-start | bytes 4718600 | tf_op jit(solution)/shard_map/ppermute | solution.py:237
  12.8 5.4 %all-to-all-start.1 = ((s32[16,1,64]{2,1,0:T(1,128)}), s32[16,1,64]{2,1,0:T(1,128)S(1)}, u32[]{:S(2)}, u32[]{:S(2)}) async-start(s32[16,1,64]{2,1,0:T(1,128)} %select_n.263), calls=%async_computation.1 | async-start | bytes 16384 | tf_op jit(solution)/shard_map/all_to_all | solution.py:256
  18.5 2.7 %slice.69 = bf16[2,512,768]{2,1,0:T(8,128)(2,1)} slice(bf16[2,512,1536]{2,1,0:T(8,128)(2,1)} %own_ref.3), slice={[0:2], [0:512], [384:1152]} | slice | bytes 3145728 | tf_op jit(solution)/shard_map/slice | solution.py:230
  24.3 10.6 %attend_local.3 = (f32[768,512]{1,0:T(8,128)S(1)}, f32[2,6,512]{2,1,0:T(8,128)S(1)}) custom-call(s32[2,6]{1,0:T(2,128)S(1)} %stack.5.bounds, bf16[512,1536]{1,0:T(8,128)(2,1)S(1)} %copy-done, bf16[2,512,1536]{2,1,0:T(8,128)(2,1)} %own_ref.3, s32[1,512]{1,0:T(1,128)S(1)} %bitcast.181, s32[512,1]{1,0:T(8,128)S(1)} %copy.163.key_seg_ref), custom_call_target="tpu_custom_call" | custom-call | flops 8589934592 | bytes 4194304 | tf_op jit(solution)/shard_map/attend_local/pallas_call | solution.py:128
  34.9 10.6 %attend_local.2 = (f32[768,512]{1,0:T(8,128)S(1)}, f32[2,6,512]{2,1,0:T(8,128)S(1)}) custom-call(s32[2,6]{1,0:T(2,128)S(1)} %stack.5.bounds, bf16[512,1536]{1,0:T(8,128)(2,1)S(1)} %copy-done, bf16[2,512,1536]{2,1,0:T(8,128)(2,1)} %own_ref.3, s32[1,512]{1,0:T(1,128)S(1)} %bitcast.182, s32[512,1]{1,0:T(8,128)S(1)} %copy.163.key_seg_ref), custom_call_target="tpu_custom_call" | custom-call | flops 8589934592 | bytes 4194304 | tf_op jit(solution)/shard_map/attend_local/pallas_call | solution.py:128
  48.8 4.4 %collective-permute-start.13 = (bf16[2,512,768]{2,1,0:T(8,128)(2,1)}, bf16[2,512,768]{2,1,0:T(8,128)(2,1)}, u32[]{:S(2)}, u32[]{:S(2)}) collective-permute-start(bf16[2,512,768]{2,1,0:T(8,128)(2,1)} %slice.69), channel_id=1, source_target_pairs={{1,0},{2,1},{3,2},{4,3},{5,4},{6,5},{7,6},{8,7},{9,8},{10,9},{11,1... | collective-permute-start | bytes 4718600 | tf_op jit(solution)/shard_map/ppermute | solution.py:237
  53.2 13.3 %attend_halo.2 = bf16[1024,768]{1,0:T(8,128)(2,1)} custom-call(s32[4,6]{1,0:T(4,128)S(1)} %stack.4.bounds, bf16[512,1536]{1,0:T(8,128)(2,1)S(1)} %copy-done, bf16[2,512,768]{2,1,0:T(8,128)(2,1)} %collective-permute-done.before_ref, bf16[2,512,768]{2,1,0:T(8,128)(2,1)} %collective-permute-done.1.after_ref, s32[1,512]{1,0:T(1,128)S(1)} %bitcast.183, ...), custom_call_target="tpu_custom_call" | custom-call | flops 17179869184 | bytes 4194304 | tf_op jit(solution)/shard_map/attend_halo/pallas_call | solution.py:160
  66.5 7.7 %all-to-all-start = ((bf16[16,64,768]{2,1,0:T(8,128)(2,1)}), bf16[16,64,768]{2,1,0:T(8,128)(2,1)}, u32[]{:S(2)}, u32[]{:S(2)}) async-start(bf16[16,64,768]{2,1,0:T(8,128)(2,1)} %bitcast.19), calls=%async_computation | async-start | bytes 3145728 | tf_op jit(solution)/shard_map/all_to_all | solution.py:291
  75.7 13.4 %attend_halo.3 = bf16[1024,768]{1,0:T(8,128)(2,1)} custom-call(s32[4,6]{1,0:T(4,128)S(1)} %stack.4.bounds, bf16[512,1536]{1,0:T(8,128)(2,1)S(1)} %copy-done, bf16[2,512,768]{2,1,0:T(8,128)(2,1)} %collective-permute-done.12.before_ref, bf16[2,512,768]{2,1,0:T(8,128)(2,1)} %collective-permute-done.13.after_ref, s32[1,512]{1,0:T(1,128)S(1)} %bitcast.184, ...), custom_call_target="tpu_custom_call" | custom-call | flops 17179869184 | bytes 4194304 | tf_op jit(solution)/shard_map/attend_halo/pallas_call | solution.py:160
  89.1 20.1 %all-to-all-done = bf16[16,64,768]{2,1,0:T(8,128)(2,1)} async-done(((bf16[16,64,768]{2,1,0:T(8,128)(2,1)}), bf16[16,64,768]{2,1,0:T(8,128)(2,1)}, u32[]{:S(2)}, u32[]{:S(2)}) %all-to-all-start) | async-done | bytes 1572896 | tf_op jit(solution)/shard_map/all_to_all | solution.py:291
  109.2 10.0 %all-to-all-start.2 = ((bf16[16,64,768]{2,1,0:T(8,128)(2,1)}), bf16[16,64,768]{2,1,0:T(8,128)(2,1)}, u32[]{:S(2)}, u32[]{:S(2)}) async-start(bf16[16,64,768]{2,1,0:T(8,128)(2,1)} %bitcast.41), calls=%async_computation.2 | async-start | bytes 3145728 | tf_op jit(solution)/shard_map/all_to_all | solution.py:291
  119.3 2.7 %fusion.32 = bf16[768,512]{1,0:T(8,128)(2,1)S(1)} fusion(bf16[1024,768]{1,0:T(8,128)(2,1)} %bitcast.20, s32[1024]{0:T(1024)S(1)} %eq.64), kind=kOutput, calls=%fused_computation.48 | convolution fusion | flops 806223872 | bytes 2363392 | tf_op jit(solution)/shard_map/sk,sr->kr/dot_general | solution.py:298
  131.1 20.1 %collective-permute-done.8 = bf16[2,96,1536]{2,1,0:T(8,128)(2,1)S(1)} collective-permute-done((bf16[2,96,1536]{2,1,0:T(8,128)(2,1)S(1)}, bf16[2,96,1536]{2,1,0:T(8,128)(2,1)S(1)}, u32[]{:S(2)}, u32[]{:S(2)}) %collective-permute-start.8) | collective-permute-done | bytes 589856 | tf_op jit(solution)/shard_map/ppermute | solution.py:224
  154.1 5.0 %collective-permute-start.10 = (bf16[96,1536]{1,0:T(8,128)(2,1)}, bf16[96,1536]{1,0:T(8,128)(2,1)}, u32[]{:S(2)}, u32[]{:S(2)}) collective-permute-start(bf16[96,1536]{1,0:T(8,128)(2,1)} %get-tuple-element.69), channel_id=1, source_target_pairs={{4,12},{5,13},{6,14},{7,15},{8,0},{9,1},{10,2},{11,3},{20,28},{21,... | collective-permute-start | bytes 884744 | tf_op jit(solution)/shard_map/ppermute | solution.py:339
  160.4 3.3 %collective-permute-start.9 = (bf16[96,1536]{1,0:T(8,128)(2,1)S(1)}, bf16[96,1536]{1,0:T(8,128)(2,1)}, u32[]{:S(2)}, u32[]{:S(2)}) collective-permute-start(bf16[96,1536]{1,0:T(8,128)(2,1)S(1)} %get-tuple-element.70), channel_id=1, source_target_pairs={{4,0},{5,1},{6,2},{7,3},{8,12},{9,13},{10,14},{11,15},{20,16},{21,... | collective-permute-start | bytes 884744 | tf_op jit(solution)/shard_map/ppermute | solution.py:339
  171.2 2.7 %fusion.33 = bf16[768,512]{1,0:T(8,128)(2,1)S(1)} fusion(bf16[1024,768]{1,0:T(8,128)(2,1)} %bitcast.42, s32[1024]{0:T(1024)S(1)} %eq.64), kind=kOutput, calls=%fused_computation.49 | convolution fusion | flops 806223872 | bytes 2363392 | tf_op jit(solution)/shard_map/sk,sr->kr/dot_general | solution.py:298
  178.3 2.3 collective-permute-start.15
  185.1 9.1 %collective-permute-done.15 = bf16[2,96,1536]{2,1,0:T(8,128)(2,1)S(1)} collective-permute-done((bf16[2,96,1536]{2,1,0:T(8,128)(2,1)S(1)}, bf16[2,96,1536]{2,1,0:T(8,128)(2,1)S(1)}, u32[]{:S(2)}, u32[]{:S(2)}) %collective-permute-start.15) | collective-permute-done | bytes 589856 | tf_op jit(solution)/shard_map/ppermute | solution.py:224
  200.8 2.9 %collective-permute-start.18 = (bf16[96,1536]{1,0:T(8,128)(2,1)S(1)}, bf16[96,1536]{1,0:T(8,128)(2,1)S(1)}, u32[]{:S(2)}, u32[]{:S(2)}) collective-permute-start(bf16[96,1536]{1,0:T(8,128)(2,1)S(1)} %get-tuple-element.63), channel_id=1, source_target_pairs={{4,8},{5,9},{6,10},{7,11},{8,4},{9,5},{10,6},{11,7},{20,24},{21,25... | collective-permute-start | bytes 884744 | tf_op jit(solution)/shard_map/ppermute | solution.py:339
  203.6 5.4 %collective-permute-done.19 = bf16[2,96,1536]{2,1,0:T(8,128)(2,1)S(1)} collective-permute-done((bf16[2,96,1536]{2,1,0:T(8,128)(2,1)S(1)}, bf16[2,96,1536]{2,1,0:T(8,128)(2,1)S(1)}, u32[]{:S(2)}, u32[]{:S(2)}) %collective-permute-start.19) | collective-permute-done | bytes 589856 | tf_op jit(solution)/shard_map/ppermute | solution.py:224
  209.1 2.1 fusion.114
  215.1 6.8 %add_convert_fusion = bf16[512,3072]{1,0:T(8,128)(2,1)} fusion(bf16[512,3072]{1,0:T(8,128)(2,1)S(1)} %copy-done.13, bf16[1536,3072]{1,0:T(8,128)(2,1)S(1)} %bitcast.209, bf16[384,512]{1,0:T(8,128)(2,1)S(1)} %copy-done.7, bf16[768,512]{1,0:T(8,128)(2,1)S(1)} %fusion.33, bf16[384,512]{1,0:T(8,128)(2,1)S(1)} %copy-done.6), kind=kOutput, calls=%fused_computation | convolution fusion | flops 4841275392 | bytes 17301504 | tf_op jit(solution)/shard_map/kr,kd->rd/dot_general | solution.py:361
  223.2 3.3 %collective-permute-start.22 = (bf16[96,1536]{1,0:T(8,128)(2,1)S(1)}, bf16[96,1536]{1,0:T(8,128)(2,1)S(1)}, u32[]{:S(2)}, u32[]{:S(2)}) collective-permute-start(bf16[96,1536]{1,0:T(8,128)(2,1)S(1)} %get-tuple-element.66), channel_id=1, source_target_pairs={{4,8},{5,9},{6,10},{7,11},{8,4},{9,5},{10,6},{11,7},{20,24},{21,25... | collective-permute-start | bytes 884744 | tf_op jit(solution)/shard_map/ppermute | solution.py:339
  227.8 6.2 %collective-permute-done.22 = bf16[96,1536]{1,0:T(8,128)(2,1)S(1)} collective-permute-done((bf16[96,1536]{1,0:T(8,128)(2,1)S(1)}, bf16[96,1536]{1,0:T(8,128)(2,1)S(1)}, u32[]{:S(2)}, u32[]{:S(2)}) %collective-permute-start.22) | collective-permute-done | bytes 294944 | tf_op jit(solution)/shard_map/ppermute | solution.py:339
  (152 shorter events, 59.4 us)
Async XLA Ops:
  3.5 43.2 %collective-permute-start = (bf16[2,512,768]{2,1,0:T(8,128)(2,1)}, bf16[2,512,768]{2,1,0:T(8,128)(2,1)}, u32[]{:S(2)}, u32[]{:S(2)}) collective-permute-start(bf16[2,512,768]{2,1,0:T(8,128)(2,1)} %pad_maximum_fusion), channel_id=1, source_target_pairs={{0,1},{1,2},{2,3},{3,4},{4,5},{5,6},{6,7},{7,8},{8,9},{9,10},{10,1... | collective-permute-start | bytes 4718600 | tf_op jit(solution)/shard_map/ppermute | solution.py:236
  5.4 41.3 %collective-permute-start.1 = (bf16[2,512,768]{2,1,0:T(8,128)(2,1)}, bf16[2,512,768]{2,1,0:T(8,128)(2,1)}, u32[]{:S(2)}, u32[]{:S(2)}) collective-permute-start(bf16[2,512,768]{2,1,0:T(8,128)(2,1)} %pad_maximum_fusion), channel_id=1, source_target_pairs={{1,0},{2,1},{3,2},{4,3},{5,4},{6,5},{7,6},{8,7},{9,8},{10,9},{11,1... | collective-permute-start | bytes 4718600 | tf_op jit(solution)/shard_map/ppermute | solution.py:237
  12.8 53.7 %all-to-all-start.1 = ((s32[16,1,64]{2,1,0:T(1,128)}), s32[16,1,64]{2,1,0:T(1,128)S(1)}, u32[]{:S(2)}, u32[]{:S(2)}) async-start(s32[16,1,64]{2,1,0:T(1,128)} %select_n.263), calls=%async_computation.1 | async-start | bytes 16384 | tf_op jit(solution)/shard_map/all_to_all | solution.py:256
  46.7 29.0 %collective-permute-start.12 = (bf16[2,512,768]{2,1,0:T(8,128)(2,1)}, bf16[2,512,768]{2,1,0:T(8,128)(2,1)}, u32[]{:S(2)}, u32[]{:S(2)}) collective-permute-start(bf16[2,512,768]{2,1,0:T(8,128)(2,1)} %slice.69), channel_id=1, source_target_pairs={{0,1},{1,2},{2,3},{3,4},{4,5},{5,6},{6,7},{7,8},{8,9},{9,10},{10,1... | collective-permute-start | bytes 4718600 | tf_op jit(solution)/shard_map/ppermute | solution.py:236
  48.8 27.0 %collective-permute-start.13 = (bf16[2,512,768]{2,1,0:T(8,128)(2,1)}, bf16[2,512,768]{2,1,0:T(8,128)(2,1)}, u32[]{:S(2)}, u32[]{:S(2)}) collective-permute-start(bf16[2,512,768]{2,1,0:T(8,128)(2,1)} %slice.69), channel_id=1, source_target_pairs={{1,0},{2,1},{3,2},{4,3},{5,4},{6,5},{7,6},{8,7},{9,8},{10,9},{11,1... | collective-permute-start | bytes 4718600 | tf_op jit(solution)/shard_map/ppermute | solution.py:237
  66.5 42.7 %all-to-all-start = ((bf16[16,64,768]{2,1,0:T(8,128)(2,1)}), bf16[16,64,768]{2,1,0:T(8,128)(2,1)}, u32[]{:S(2)}, u32[]{:S(2)}) async-start(bf16[16,64,768]{2,1,0:T(8,128)(2,1)} %bitcast.19), calls=%async_computation | async-start | bytes 3145728 | tf_op jit(solution)/shard_map/all_to_all | solution.py:291
  74.3 50.4 %collective-permute-start.3 = (bf16[512,3072]{1,0:T(8,128)(2,1)}, bf16[512,3072]{1,0:T(8,128)(2,1)}, u32[]{:S(2)}, u32[]{:S(2)}) collective-permute-start(bf16[512,3072]{1,0:T(8,128)(2,1)} %param.15), channel_id=1, source_target_pairs={{0,1},{1,0},{2,3},{3,2},{4,5},{5,4},{6,7},{7,6},{8,9},{9,8},{10,11... | collective-permute-start | bytes 9437192 | tf_op jit(solution)/shard_map/ppermute | solution.py:224
  109.2 61.9 %all-to-all-start.2 = ((bf16[16,64,768]{2,1,0:T(8,128)(2,1)}), bf16[16,64,768]{2,1,0:T(8,128)(2,1)}, u32[]{:S(2)}, u32[]{:S(2)}) async-start(bf16[16,64,768]{2,1,0:T(8,128)(2,1)} %bitcast.41), calls=%async_computation.2 | async-start | bytes 3145728 | tf_op jit(solution)/shard_map/all_to_all | solution.py:291
  126.6 24.7 %collective-permute-start.8 = (bf16[2,96,1536]{2,1,0:T(8,128)(2,1)S(1)}, bf16[2,96,1536]{2,1,0:T(8,128)(2,1)S(1)}, u32[]{:S(2)}, u32[]{:S(2)}) collective-permute-start(bf16[2,96,1536]{2,1,0:T(8,128)(2,1)S(1)} %fusion.5), channel_id=1, source_target_pairs={{0,2},{1,3},{2,0},{3,1},{4,6},{5,7},{6,4},{7,5},{8,10},{9,11},{10,... | collective-permute-start | bytes 1769480 | tf_op jit(solution)/shard_map/ppermute | solution.py:224
  130.5 34.9 %collective-permute-start.4 = (bf16[2,96,1536]{2,1,0:T(8,128)(2,1)S(1)}, bf16[2,96,1536]{2,1,0:T(8,128)(2,1)S(1)}, u32[]{:S(2)}, u32[]{:S(2)}) collective-permute-start(bf16[2,96,1536]{2,1,0:T(8,128)(2,1)S(1)} %fusion.4), channel_id=1, source_target_pairs={{0,2},{1,3},{2,0},{3,1},{4,6},{5,7},{6,4},{7,5},{8,10},{9,11},{10,... | collective-permute-start | bytes 1769480 | tf_op jit(solution)/shard_map/ppermute | solution.py:224
  154.1 29.0 %collective-permute-start.10 = (bf16[96,1536]{1,0:T(8,128)(2,1)}, bf16[96,1536]{1,0:T(8,128)(2,1)}, u32[]{:S(2)}, u32[]{:S(2)}) collective-permute-start(bf16[96,1536]{1,0:T(8,128)(2,1)} %get-tuple-element.69), channel_id=1, source_target_pairs={{4,12},{5,13},{6,14},{7,15},{8,0},{9,1},{10,2},{11,3},{20,28},{21,... | collective-permute-start | bytes 884744 | tf_op jit(solution)/shard_map/ppermute | solution.py:339
  159.0 25.3 %collective-permute-start.11 = (bf16[96,1536]{1,0:T(8,128)(2,1)}, bf16[96,1536]{1,0:T(8,128)(2,1)}, u32[]{:S(2)}, u32[]{:S(2)}) collective-permute-start(bf16[96,1536]{1,0:T(8,128)(2,1)} %get-tuple-element.68), channel_id=1, source_target_pairs={{0,12},{1,13},{2,14},{3,15},{12,0},{13,1},{14,2},{15,3},{16,28},{1... | collective-permute-start | bytes 884744 | tf_op jit(solution)/shard_map/ppermute | solution.py:339
  160.4 37.4 %collective-permute-start.9 = (bf16[96,1536]{1,0:T(8,128)(2,1)S(1)}, bf16[96,1536]{1,0:T(8,128)(2,1)}, u32[]{:S(2)}, u32[]{:S(2)}) collective-permute-start(bf16[96,1536]{1,0:T(8,128)(2,1)S(1)} %get-tuple-element.70), channel_id=1, source_target_pairs={{4,0},{5,1},{6,2},{7,3},{8,12},{9,13},{10,14},{11,15},{20,16},{21,... | collective-permute-start | bytes 884744 | tf_op jit(solution)/shard_map/ppermute | solution.py:339
  168.2 29.6 %collective-permute-start.5 = (bf16[96,1536]{1,0:T(8,128)(2,1)}, bf16[96,1536]{1,0:T(8,128)(2,1)}, u32[]{:S(2)}, u32[]{:S(2)}) collective-permute-start(bf16[96,1536]{1,0:T(8,128)(2,1)} %get-tuple-element.73), channel_id=1, source_target_pairs={{4,0},{5,1},{6,2},{7,3},{8,12},{9,13},{10,14},{11,15},{20,16},{21,... | collective-permute-start | bytes 884744 | tf_op jit(solution)/shard_map/ppermute | solution.py:339
  178.3 15.9 %collective-permute-start.15 = (bf16[2,96,1536]{2,1,0:T(8,128)(2,1)S(1)}, bf16[2,96,1536]{2,1,0:T(8,128)(2,1)S(1)}, u32[]{:S(2)}, u32[]{:S(2)}) collective-permute-start(bf16[2,96,1536]{2,1,0:T(8,128)(2,1)S(1)} %fusion.6), channel_id=1, source_target_pairs={{0,2},{1,3},{2,0},{3,1},{4,6},{5,7},{6,4},{7,5},{8,10},{9,11},{10,... | collective-permute-start | bytes 1769480 | tf_op jit(solution)/shard_map/ppermute | solution.py:224
  183.1 14.8 %collective-permute-start.6 = (bf16[96,1536]{1,0:T(8,128)(2,1)S(1)}, bf16[96,1536]{1,0:T(8,128)(2,1)S(1)}, u32[]{:S(2)}, u32[]{:S(2)}) collective-permute-start(bf16[96,1536]{1,0:T(8,128)(2,1)S(1)} %copy-done.10), channel_id=1, source_target_pairs={{4,12},{5,13},{6,14},{7,15},{8,0},{9,1},{10,2},{11,3},{20,28},{21,... | collective-permute-start | bytes 884744 | tf_op jit(solution)/shard_map/ppermute | solution.py:339
  184.4 13.5 %collective-permute-start.7 = (bf16[96,1536]{1,0:T(8,128)(2,1)S(1)}, bf16[96,1536]{1,0:T(8,128)(2,1)S(1)}, u32[]{:S(2)}, u32[]{:S(2)}) collective-permute-start(bf16[96,1536]{1,0:T(8,128)(2,1)S(1)} %copy-done.9), channel_id=1, source_target_pairs={{0,12},{1,13},{2,14},{3,15},{12,0},{13,1},{14,2},{15,3},{16,28},{1... | collective-permute-start | bytes 884744 | tf_op jit(solution)/shard_map/ppermute | solution.py:339
  194.2 14.9 %collective-permute-start.19 = (bf16[2,96,1536]{2,1,0:T(8,128)(2,1)S(1)}, bf16[2,96,1536]{2,1,0:T(8,128)(2,1)S(1)}, u32[]{:S(2)}, u32[]{:S(2)}) collective-permute-start(bf16[2,96,1536]{2,1,0:T(8,128)(2,1)S(1)} %fusion.7), channel_id=1, source_target_pairs={{0,2},{1,3},{2,0},{3,1},{4,6},{5,7},{6,4},{7,5},{8,10},{9,11},{10,... | collective-permute-start | bytes 1769480 | tf_op jit(solution)/shard_map/ppermute | solution.py:224
  198.0 25.1 %collective-permute-start.16 = (bf16[96,1536]{1,0:T(8,128)(2,1)S(1)}, bf16[96,1536]{1,0:T(8,128)(2,1)S(1)}, u32[]{:S(2)}, u32[]{:S(2)}) collective-permute-start(bf16[96,1536]{1,0:T(8,128)(2,1)S(1)} %get-tuple-element.62), channel_id=1, source_target_pairs={{0,4},{1,5},{2,6},{3,7},{12,8},{13,9},{14,10},{15,11},{16,20},{17,... | collective-permute-start | bytes 884744 | tf_op jit(solution)/shard_map/ppermute | solution.py:339
  199.5 27.0 %collective-permute-start.17 = (bf16[96,1536]{1,0:T(8,128)(2,1)S(1)}, bf16[96,1536]{1,0:T(8,128)(2,1)S(1)}, u32[]{:S(2)}, u32[]{:S(2)}) collective-permute-start(bf16[96,1536]{1,0:T(8,128)(2,1)S(1)} %get-tuple-element.64), channel_id=1, source_target_pairs={{0,8},{1,9},{2,10},{3,11},{12,4},{13,5},{14,6},{15,7},{16,24},{17,... | collective-permute-start | bytes 884744 | tf_op jit(solution)/shard_map/ppermute | solution.py:339
  200.8 25.7 %collective-permute-start.18 = (bf16[96,1536]{1,0:T(8,128)(2,1)S(1)}, bf16[96,1536]{1,0:T(8,128)(2,1)S(1)}, u32[]{:S(2)}, u32[]{:S(2)}) collective-permute-start(bf16[96,1536]{1,0:T(8,128)(2,1)S(1)} %get-tuple-element.63), channel_id=1, source_target_pairs={{4,8},{5,9},{6,10},{7,11},{8,4},{9,5},{10,6},{11,7},{20,24},{21,25... | collective-permute-start | bytes 884744 | tf_op jit(solution)/shard_map/ppermute | solution.py:339
  211.2 15.4 %collective-permute-start.20 = (bf16[96,1536]{1,0:T(8,128)(2,1)S(1)}, bf16[96,1536]{1,0:T(8,128)(2,1)S(1)}, u32[]{:S(2)}, u32[]{:S(2)}) collective-permute-start(bf16[96,1536]{1,0:T(8,128)(2,1)S(1)} %get-tuple-element.65), channel_id=1, source_target_pairs={{0,4},{1,5},{2,6},{3,7},{12,8},{13,9},{14,10},{15,11},{16,20},{17,... | collective-permute-start | bytes 884744 | tf_op jit(solution)/shard_map/ppermute | solution.py:339
  212.7 15.2 %collective-permute-start.21 = (bf16[96,1536]{1,0:T(8,128)(2,1)S(1)}, bf16[96,1536]{1,0:T(8,128)(2,1)S(1)}, u32[]{:S(2)}, u32[]{:S(2)}) collective-permute-start(bf16[96,1536]{1,0:T(8,128)(2,1)S(1)} %get-tuple-element.67), channel_id=1, source_target_pairs={{0,8},{1,9},{2,10},{3,11},{12,4},{13,5},{14,6},{15,7},{16,24},{17,... | collective-permute-start | bytes 884744 | tf_op jit(solution)/shard_map/ppermute | solution.py:339
  223.2 10.9 %collective-permute-start.22 = (bf16[96,1536]{1,0:T(8,128)(2,1)S(1)}, bf16[96,1536]{1,0:T(8,128)(2,1)S(1)}, u32[]{:S(2)}, u32[]{:S(2)}) collective-permute-start(bf16[96,1536]{1,0:T(8,128)(2,1)S(1)} %get-tuple-element.66), channel_id=1, source_target_pairs={{4,8},{5,9},{6,10},{7,11},{8,4},{9,5},{10,6},{11,7},{20,24},{21,25... | collective-permute-start | bytes 884744 | tf_op jit(solution)/shard_map/ppermute | solution.py:339
  (19 other events, 177.6 us)
